TPU v7x, 256 devices: a whole 4x4x8 slice. The times are simulated.
256 devices in a mesh: lat: 16 (over z, x_lo), lon: 16 (over x_hi, y, core).
Axes of the slice: x: 4 (x_hi: 2, x_lo: 2; x = x_hi * 2 + x_lo), y: 4, z: 8, core: 2. Of those that a mesh axis runs over, the one named last changes fastest.
Arguments:
- tokens: bfloat16 [128, 256, 2, 1024], P('lat', 'lon'), may hold values from -6 to 6
- norm_gain: bfloat16 [1024], replicated, may hold values from 0.099609375 to 1.8984375
- q_weight: bfloat16 [1024, 1024], replicated, may hold values from -3 to 3
- k_weight: bfloat16 [1024, 1024], replicated, may hold values from -3 to 3
- v_weight: bfloat16 [1024, 1024], replicated, may hold values from -0.1875 to 0.1875
- o_weight: bfloat16 [1024, 1024], replicated, may hold values from -0.75 to 0.75
- band_start: int32 [16], replicated, may hold values from -15 to 0, as said below
- band_width: int32 [16], replicated, may hold values from 2 to 16, as said below
Outputs:
- mixed: bfloat16 [128, 256, 2, 1024], P('lat', 'lon')
Inputs may be any that keep to these rules, and one draw needn't show every extreme that they name: `band_width`: band 0 and band 16 - 1 have width 16; widths need not grow band by band. 1 - band_width[b] <= band_start[b], so a query's own block is always seen.
All inputs are finite; a program needn't handle non-finite values.
Results may differ from a plain program's by a relative error of at most 0.006.
Values may be sent and summed in bfloat16 or wider, within the bound.
No kernel may reach another device: no remote copies, remote signals or barrier semaphores. Data moves between devices by JAX's collectives and lax.ppermute only.
A program may use at most 128 MiB of HBM per device.

v0:
```python
import jax
import jax.numpy as jnp
from jax import lax
from jax.sharding import PartitionSpec as P

HD = 64


def with_halo(array, sides, width):
    for axis, dim in sides:
        devices, length = (lax.axis_size(axis), array.shape[dim])
        up = [(i, (i + 1) % devices) for i in range(devices - 1)]
        down = [(j, i) for i, j in up]
        last = lax.slice_in_dim(array, length - width, length, axis=dim)
        leading = lax.slice_in_dim(array, 0, width, axis=dim)
        before = lax.ppermute(last, axis, up)
        after = lax.ppermute(leading, axis, down)
        array = jnp.concatenate([before, array, after], axis=dim)
    return array


def from_behind(value, axis, steps):
    count = lax.axis_size(axis)
    pairs = [(source, (source + steps) % count) for source in range(count)]
    return lax.ppermute(value, axis, pairs)


def body(tokens, norm_gain, q_weight, k_weight, v_weight, o_weight, band_start, band_width):
    rows, columns, levels, width = tokens.shape
    heads = width // HD
    n_lon = lax.axis_size("lon")
    n_lat = lax.axis_size("lat")
    band = lax.axis_index("lat")
    block = lax.axis_index("lon")
    wide = tokens.astype(jnp.float32)
    normed = (
        wide
        * lax.rsqrt(jnp.mean(wide * wide, -1, keepdims=True) + 1e-06)
        * norm_gain.astype(jnp.float32)
    ).astype(jnp.bfloat16)
    flat = normed.reshape(-1, width)
    query = jnp.dot(flat, q_weight, preferred_element_type=jnp.float32).astype(jnp.bfloat16)
    keys = jnp.dot(flat, k_weight, preferred_element_type=jnp.float32).astype(jnp.bfloat16)
    values = jnp.dot(flat, v_weight, preferred_element_type=jnp.float32).astype(jnp.bfloat16)
    query_heads = query.reshape(-1, heads, HD)
    count_queries = query_heads.shape[0]
    pair = jnp.stack(
        [keys.reshape(rows, columns, levels, width), values.reshape(rows, columns, levels, width)]
    )
    padded = with_halo(pair, (("lat", 1),), 1)
    edges = jnp.stack([pair[:, 0], pair[:, rows - 1]], axis=1)
    across = from_behind(edges, "lon", n_lon // 2)
    top_row = across[:, 0]
    bottom_row = across[:, 1]
    first = jnp.where(band == 0, top_row, padded[:, 0])
    last = jnp.where(band == n_lat - 1, bottom_row, padded[:, rows + 1])
    extended = jnp.concatenate([first[:, None], padded[:, 1 : rows + 1], last[:, None]], axis=1)
    start_here = band_start[band]
    span_here = band_width[band]
    scale = HD ** (-0.5)

    def attend(state, piece, owner):
        inside = jnp.mod(owner - block - start_here, n_lon) < span_here

        def update(carry):
            top, total, weighted = carry
            key_heads = piece[0].reshape(-1, heads, HD)
            value_heads = piece[1].reshape(-1, heads, HD)
            scores = (
                jnp.einsum(
                    "qhd,khd->hqk", query_heads, key_heads, preferred_element_type=jnp.float32
                )
                * scale
            )
            new_top = jnp.maximum(top, jnp.max(scores, -1))
            raw = jnp.exp(scores - new_top[..., None])
            fade = jnp.exp(top - new_top)
            total = total * fade + jnp.sum(raw, -1)
            weighted = weighted * fade[..., None] + jnp.einsum(
                "hqk,khd->hqd",
                raw.astype(jnp.bfloat16),
                value_heads,
                preferred_element_type=jnp.float32,
            )
            return (new_top, total, weighted)

        def keep(carry):
            return carry

        return lax.cond(inside, update, keep, state)

    initial = (
        jnp.full((heads, count_queries), -1e30, jnp.float32),
        jnp.zeros((heads, count_queries), jnp.float32),
        jnp.zeros((heads, count_queries, HD), jnp.float32),
    )
    carry = initial
    piece = lax.all_gather(extended, "lon", axis=2, tiled=True)
    count = piece.shape[2] // columns
    split = jnp.moveaxis(piece.reshape(2, rows + 2, count, columns, levels, width), 2, 0)

    def advance(inner, element):
        single, offset = element
        return (attend(inner, single, offset), None)

    carry, unused = lax.scan(advance, carry, (split, jnp.arange(count, dtype=jnp.int32)))
    state = carry
    top, total, weighted = state
    attended = (
        (weighted / total[..., None]).transpose(1, 0, 2).reshape(-1, width).astype(jnp.bfloat16)
    )
    mixed = wide.reshape(-1, width) + jnp.dot(
        attended, o_weight, preferred_element_type=jnp.float32
    )
    return mixed.astype(jnp.bfloat16).reshape(rows, columns, levels, width)


def solution(mesh):
    placed = (P("lat", "lon", None, None), P(), P(), P(), P(), P(), P(), P())
    return jax.shard_map(
        body, mesh=mesh, in_specs=placed, out_specs=P("lat", "lon", None, None), check_vma=False
    )
```

profile of v0, /device:TPU:1, one launch (start us, length us, event | category | flops | bytes accessed | tf_op | source)
XLA Modules:
  0.0 453.6 jit_solution(10605950701415543880)
XLA Ops:
  33.7 134.1 %all-gather.2.cloned.1.call-done = bf16[2,10,256,2,1024]{4,2,3,1,0:T(8,128)(2,1)} async-done(((bf16[2,10,16,2,1024]{4,2,3,1,0:T(8,128)(2,1)}), bf16[2,10,256,2,1024]{4,2,3,1,0:T(8,128)(2,1)}) %all-gather.2.cloned.1.call-update) | async-done | bytes 20971536 | tf_op jit(solution)/shard_map/all_gather | solution.py:98
  167.8 38.5 %copy.30 = bf16[16,2,10,16,2,1024]{5,4,3,2,1,0:T(2,128)(2,1)} copy(bf16[16,2,10,16,2,1024]{5,3,0,4,2,1:T(8,128)(2,1)} %bitcast.33) | data formatting | bytes 41943040 | tf_op jit(solution)/shard_map/while | solution.py:106
  207.4 234.3 %while.16 = (s32[]{:T(128)}, f32[16,256]{1,0:T(8,128)S(1)}, f32[16,256]{1,0:T(8,128)S(1)}, f32[16,256,64]{1,2,0:T(8,128)}, s32[16]{0:T(128)S(1)}, /*index=5*/s32...) while((s32[]{:T(128)}, f32[16,256]{1,0:T(8,128)S(1)}, ...), condition=%wide.region_6.7_spmd, body=%wide.region_1.6_spmd.sunk | while | flops 346562560 | bytes 46137788 | solution.py:106
  209.8 12.3 %conditional.2 = ((f32[16,256]{1,0:T(8,128)S(1)}, f32[16,256]{1,0:T(8,128)S(1)}, f32[16,256,64]{1,2,0:T(8,128)})) conditional(s32[]{:T(128)} %convert_element_type.63, (f32[16,256]{1,0:T(8,128)S(1)}, f32[16,256]{1,0:T(8,128)S(1)}, f32[16,256,64]{1,2,0:T(8,128)}) %tuple.46, (bf16[16,2,10,16,2,1024]{5,4,3,2,1,0:T(2,128)(2,1)}, s32[]{:T(128)}, ...), branch_computations={%region_2.2_spmd, %region_3.5_spmd} | conditional | flops 346562560 | bytes 46137424 | solution.py:90
  217.1 4.9 %fusion.7 = f32[16,256,64]{1,2,0:T(8,128)} fusion(f32[16,320,256]{2,1,0:T(8,128)} %copy-done.2, f32[16,256]{1,0:T(8,128)S(1)} %max.3, bf16[320,16,64]{2,1,0:T(8,128)(2,1)S(1)} %squeeze.25, f32[16,256,64]{1,2,0:T(8,128)} %get-tuple-element.163, f32[16,256]{1,0:T(8,128)S(1)} %get-tuple-element.243), kind=kOutput, calls=%fused_computation.8 | convolution fusion | flops 172228608 | bytes 8028160 | tf_op jit(solution)/shard_map/while/body/eval_jaxpr/cond/branch_1_fun/hqk,khd->hqd/dot_general | solution.py:79
  224.4 12.3 %conditional.2 = ((f32[16,256]{1,0:T(8,128)S(1)}, f32[16,256]{1,0:T(8,128)S(1)}, f32[16,256,64]{1,2,0:T(8,128)})) conditional(s32[]{:T(128)} %convert_element_type.63, (f32[16,256]{1,0:T(8,128)S(1)}, f32[16,256]{1,0:T(8,128)S(1)}, f32[16,256,64]{1,2,0:T(8,128)}) %tuple.46, (bf16[16,2,10,16,2,1024]{5,4,3,2,1,0:T(2,128)(2,1)}, s32[]{:T(128)}, ...), branch_computations={%region_2.2_spmd, %region_3.5_spmd} | conditional | flops 346562560 | bytes 46137424 | solution.py:90
  231.8 4.9 %fusion.7 = f32[16,256,64]{1,2,0:T(8,128)} fusion(f32[16,320,256]{2,1,0:T(8,128)} %copy-done.2, f32[16,256]{1,0:T(8,128)S(1)} %max.3, bf16[320,16,64]{2,1,0:T(8,128)(2,1)S(1)} %squeeze.25, f32[16,256,64]{1,2,0:T(8,128)} %get-tuple-element.163, f32[16,256]{1,0:T(8,128)S(1)} %get-tuple-element.243), kind=kOutput, calls=%fused_computation.8 | convolution fusion | flops 172228608 | bytes 8028160 | tf_op jit(solution)/shard_map/while/body/eval_jaxpr/cond/branch_1_fun/hqk,khd->hqd/dot_general | solution.py:79
  239.1 12.3 %conditional.2 = ((f32[16,256]{1,0:T(8,128)S(1)}, f32[16,256]{1,0:T(8,128)S(1)}, f32[16,256,64]{1,2,0:T(8,128)})) conditional(s32[]{:T(128)} %convert_element_type.63, (f32[16,256]{1,0:T(8,128)S(1)}, f32[16,256]{1,0:T(8,128)S(1)}, f32[16,256,64]{1,2,0:T(8,128)}) %tuple.46, (bf16[16,2,10,16,2,1024]{5,4,3,2,1,0:T(2,128)(2,1)}, s32[]{:T(128)}, ...), branch_computations={%region_2.2_spmd, %region_3.5_spmd} | conditional | flops 346562560 | bytes 46137424 | solution.py:90
  246.4 4.9 %fusion.7 = f32[16,256,64]{1,2,0:T(8,128)} fusion(f32[16,320,256]{2,1,0:T(8,128)} %copy-done.2, f32[16,256]{1,0:T(8,128)S(1)} %max.3, bf16[320,16,64]{2,1,0:T(8,128)(2,1)S(1)} %squeeze.25, f32[16,256,64]{1,2,0:T(8,128)} %get-tuple-element.163, f32[16,256]{1,0:T(8,128)S(1)} %get-tuple-element.243), kind=kOutput, calls=%fused_computation.8 | convolution fusion | flops 172228608 | bytes 8028160 | tf_op jit(solution)/shard_map/while/body/eval_jaxpr/cond/branch_1_fun/hqk,khd->hqd/dot_general | solution.py:79
  253.7 12.3 %conditional.2 = ((f32[16,256]{1,0:T(8,128)S(1)}, f32[16,256]{1,0:T(8,128)S(1)}, f32[16,256,64]{1,2,0:T(8,128)})) conditional(s32[]{:T(128)} %convert_element_type.63, (f32[16,256]{1,0:T(8,128)S(1)}, f32[16,256]{1,0:T(8,128)S(1)}, f32[16,256,64]{1,2,0:T(8,128)}) %tuple.46, (bf16[16,2,10,16,2,1024]{5,4,3,2,1,0:T(2,128)(2,1)}, s32[]{:T(128)}, ...), branch_computations={%region_2.2_spmd, %region_3.5_spmd} | conditional | flops 346562560 | bytes 46137424 | solution.py:90
  261.1 4.9 %fusion.7 = f32[16,256,64]{1,2,0:T(8,128)} fusion(f32[16,320,256]{2,1,0:T(8,128)} %copy-done.2, f32[16,256]{1,0:T(8,128)S(1)} %max.3, bf16[320,16,64]{2,1,0:T(8,128)(2,1)S(1)} %squeeze.25, f32[16,256,64]{1,2,0:T(8,128)} %get-tuple-element.163, f32[16,256]{1,0:T(8,128)S(1)} %get-tuple-element.243), kind=kOutput, calls=%fused_computation.8 | convolution fusion | flops 172228608 | bytes 8028160 | tf_op jit(solution)/shard_map/while/body/eval_jaxpr/cond/branch_1_fun/hqk,khd->hqd/dot_general | solution.py:79
  268.4 12.3 %conditional.2 = ((f32[16,256]{1,0:T(8,128)S(1)}, f32[16,256]{1,0:T(8,128)S(1)}, f32[16,256,64]{1,2,0:T(8,128)})) conditional(s32[]{:T(128)} %convert_element_type.63, (f32[16,256]{1,0:T(8,128)S(1)}, f32[16,256]{1,0:T(8,128)S(1)}, f32[16,256,64]{1,2,0:T(8,128)}) %tuple.46, (bf16[16,2,10,16,2,1024]{5,4,3,2,1,0:T(2,128)(2,1)}, s32[]{:T(128)}, ...), branch_computations={%region_2.2_spmd, %region_3.5_spmd} | conditional | flops 346562560 | bytes 46137424 | solution.py:90
  275.7 4.9 %fusion.7 = f32[16,256,64]{1,2,0:T(8,128)} fusion(f32[16,320,256]{2,1,0:T(8,128)} %copy-done.2, f32[16,256]{1,0:T(8,128)S(1)} %max.3, bf16[320,16,64]{2,1,0:T(8,128)(2,1)S(1)} %squeeze.25, f32[16,256,64]{1,2,0:T(8,128)} %get-tuple-element.163, f32[16,256]{1,0:T(8,128)S(1)} %get-tuple-element.243), kind=kOutput, calls=%fused_computation.8 | convolution fusion | flops 172228608 | bytes 8028160 | tf_op jit(solution)/shard_map/while/body/eval_jaxpr/cond/branch_1_fun/hqk,khd->hqd/dot_general | solution.py:79
  283.0 12.3 %conditional.2 = ((f32[16,256]{1,0:T(8,128)S(1)}, f32[16,256]{1,0:T(8,128)S(1)}, f32[16,256,64]{1,2,0:T(8,128)})) conditional(s32[]{:T(128)} %convert_element_type.63, (f32[16,256]{1,0:T(8,128)S(1)}, f32[16,256]{1,0:T(8,128)S(1)}, f32[16,256,64]{1,2,0:T(8,128)}) %tuple.46, (bf16[16,2,10,16,2,1024]{5,4,3,2,1,0:T(2,128)(2,1)}, s32[]{:T(128)}, ...), branch_computations={%region_2.2_spmd, %region_3.5_spmd} | conditional | flops 346562560 | bytes 46137424 | solution.py:90
  297.6 12.3 %conditional.2 = ((f32[16,256]{1,0:T(8,128)S(1)}, f32[16,256]{1,0:T(8,128)S(1)}, f32[16,256,64]{1,2,0:T(8,128)})) conditional(s32[]{:T(128)} %convert_element_type.63, (f32[16,256]{1,0:T(8,128)S(1)}, f32[16,256]{1,0:T(8,128)S(1)}, f32[16,256,64]{1,2,0:T(8,128)}) %tuple.46, (bf16[16,2,10,16,2,1024]{5,4,3,2,1,0:T(2,128)(2,1)}, s32[]{:T(128)}, ...), branch_computations={%region_2.2_spmd, %region_3.5_spmd} | conditional | flops 346562560 | bytes 46137424 | solution.py:90
  305.0 4.9 %fusion.7 = f32[16,256,64]{1,2,0:T(8,128)} fusion(f32[16,320,256]{2,1,0:T(8,128)} %copy-done.2, f32[16,256]{1,0:T(8,128)S(1)} %max.3, bf16[320,16,64]{2,1,0:T(8,128)(2,1)S(1)} %squeeze.25, f32[16,256,64]{1,2,0:T(8,128)} %get-tuple-element.163, f32[16,256]{1,0:T(8,128)S(1)} %get-tuple-element.243), kind=kOutput, calls=%fused_computation.8 | convolution fusion | flops 172228608 | bytes 8028160 | tf_op jit(solution)/shard_map/while/body/eval_jaxpr/cond/branch_1_fun/hqk,khd->hqd/dot_general | solution.py:79
  312.3 12.3 %conditional.2 = ((f32[16,256]{1,0:T(8,128)S(1)}, f32[16,256]{1,0:T(8,128)S(1)}, f32[16,256,64]{1,2,0:T(8,128)})) conditional(s32[]{:T(128)} %convert_element_type.63, (f32[16,256]{1,0:T(8,128)S(1)}, f32[16,256]{1,0:T(8,128)S(1)}, f32[16,256,64]{1,2,0:T(8,128)}) %tuple.46, (bf16[16,2,10,16,2,1024]{5,4,3,2,1,0:T(2,128)(2,1)}, s32[]{:T(128)}, ...), branch_computations={%region_2.2_spmd, %region_3.5_spmd} | conditional | flops 346562560 | bytes 46137424 | solution.py:90
  326.9 12.3 %conditional.2 = ((f32[16,256]{1,0:T(8,128)S(1)}, f32[16,256]{1,0:T(8,128)S(1)}, f32[16,256,64]{1,2,0:T(8,128)})) conditional(s32[]{:T(128)} %convert_element_type.63, (f32[16,256]{1,0:T(8,128)S(1)}, f32[16,256]{1,0:T(8,128)S(1)}, f32[16,256,64]{1,2,0:T(8,128)}) %tuple.46, (bf16[16,2,10,16,2,1024]{5,4,3,2,1,0:T(2,128)(2,1)}, s32[]{:T(128)}, ...), branch_computations={%region_2.2_spmd, %region_3.5_spmd} | conditional | flops 346562560 | bytes 46137424 | solution.py:90
  334.3 4.9 %fusion.7 = f32[16,256,64]{1,2,0:T(8,128)} fusion(f32[16,320,256]{2,1,0:T(8,128)} %copy-done.2, f32[16,256]{1,0:T(8,128)S(1)} %max.3, bf16[320,16,64]{2,1,0:T(8,128)(2,1)S(1)} %squeeze.25, f32[16,256,64]{1,2,0:T(8,128)} %get-tuple-element.163, f32[16,256]{1,0:T(8,128)S(1)} %get-tuple-element.243), kind=kOutput, calls=%fused_computation.8 | convolution fusion | flops 172228608 | bytes 8028160 | tf_op jit(solution)/shard_map/while/body/eval_jaxpr/cond/branch_1_fun/hqk,khd->hqd/dot_general | solution.py:79
  341.6 12.3 %conditional.2 = ((f32[16,256]{1,0:T(8,128)S(1)}, f32[16,256]{1,0:T(8,128)S(1)}, f32[16,256,64]{1,2,0:T(8,128)})) conditional(s32[]{:T(128)} %convert_element_type.63, (f32[16,256]{1,0:T(8,128)S(1)}, f32[16,256]{1,0:T(8,128)S(1)}, f32[16,256,64]{1,2,0:T(8,128)}) %tuple.46, (bf16[16,2,10,16,2,1024]{5,4,3,2,1,0:T(2,128)(2,1)}, s32[]{:T(128)}, ...), branch_computations={%region_2.2_spmd, %region_3.5_spmd} | conditional | flops 346562560 | bytes 46137424 | solution.py:90
  356.2 12.3 %conditional.2 = ((f32[16,256]{1,0:T(8,128)S(1)}, f32[16,256]{1,0:T(8,128)S(1)}, f32[16,256,64]{1,2,0:T(8,128)})) conditional(s32[]{:T(128)} %convert_element_type.63, (f32[16,256]{1,0:T(8,128)S(1)}, f32[16,256]{1,0:T(8,128)S(1)}, f32[16,256,64]{1,2,0:T(8,128)}) %tuple.46, (bf16[16,2,10,16,2,1024]{5,4,3,2,1,0:T(2,128)(2,1)}, s32[]{:T(128)}, ...), branch_computations={%region_2.2_spmd, %region_3.5_spmd} | conditional | flops 346562560 | bytes 46137424 | solution.py:90
  363.6 4.9 %fusion.7 = f32[16,256,64]{1,2,0:T(8,128)} fusion(f32[16,320,256]{2,1,0:T(8,128)} %copy-done.2, f32[16,256]{1,0:T(8,128)S(1)} %max.3, bf16[320,16,64]{2,1,0:T(8,128)(2,1)S(1)} %squeeze.25, f32[16,256,64]{1,2,0:T(8,128)} %get-tuple-element.163, f32[16,256]{1,0:T(8,128)S(1)} %get-tuple-element.243), kind=kOutput, calls=%fused_computation.8 | convolution fusion | flops 172228608 | bytes 8028160 | tf_op jit(solution)/shard_map/while/body/eval_jaxpr/cond/branch_1_fun/hqk,khd->hqd/dot_general | solution.py:79
  370.9 12.3 %conditional.2 = ((f32[16,256]{1,0:T(8,128)S(1)}, f32[16,256]{1,0:T(8,128)S(1)}, f32[16,256,64]{1,2,0:T(8,128)})) conditional(s32[]{:T(128)} %convert_element_type.63, (f32[16,256]{1,0:T(8,128)S(1)}, f32[16,256]{1,0:T(8,128)S(1)}, f32[16,256,64]{1,2,0:T(8,128)}) %tuple.46, (bf16[16,2,10,16,2,1024]{5,4,3,2,1,0:T(2,128)(2,1)}, s32[]{:T(128)}, ...), branch_computations={%region_2.2_spmd, %region_3.5_spmd} | conditional | flops 346562560 | bytes 46137424 | solution.py:90
  378.2 4.9 %fusion.7 = f32[16,256,64]{1,2,0:T(8,128)} fusion(f32[16,320,256]{2,1,0:T(8,128)} %copy-done.2, f32[16,256]{1,0:T(8,128)S(1)} %max.3, bf16[320,16,64]{2,1,0:T(8,128)(2,1)S(1)} %squeeze.25, f32[16,256,64]{1,2,0:T(8,128)} %get-tuple-element.163, f32[16,256]{1,0:T(8,128)S(1)} %get-tuple-element.243), kind=kOutput, calls=%fused_computation.8 | convolution fusion | flops 172228608 | bytes 8028160 | tf_op jit(solution)/shard_map/while/body/eval_jaxpr/cond/branch_1_fun/hqk,khd->hqd/dot_general | solution.py:79
  385.5 12.3 %conditional.2 = ((f32[16,256]{1,0:T(8,128)S(1)}, f32[16,256]{1,0:T(8,128)S(1)}, f32[16,256,64]{1,2,0:T(8,128)})) conditional(s32[]{:T(128)} %convert_element_type.63, (f32[16,256]{1,0:T(8,128)S(1)}, f32[16,256]{1,0:T(8,128)S(1)}, f32[16,256,64]{1,2,0:T(8,128)}) %tuple.46, (bf16[16,2,10,16,2,1024]{5,4,3,2,1,0:T(2,128)(2,1)}, s32[]{:T(128)}, ...), branch_computations={%region_2.2_spmd, %region_3.5_spmd} | conditional | flops 346562560 | bytes 46137424 | solution.py:90
  392.9 4.9 %fusion.7 = f32[16,256,64]{1,2,0:T(8,128)} fusion(f32[16,320,256]{2,1,0:T(8,128)} %copy-done.2, f32[16,256]{1,0:T(8,128)S(1)} %max.3, bf16[320,16,64]{2,1,0:T(8,128)(2,1)S(1)} %squeeze.25, f32[16,256,64]{1,2,0:T(8,128)} %get-tuple-element.163, f32[16,256]{1,0:T(8,128)S(1)} %get-tuple-element.243), kind=kOutput, calls=%fused_computation.8 | convolution fusion | flops 172228608 | bytes 8028160 | tf_op jit(solution)/shard_map/while/body/eval_jaxpr/cond/branch_1_fun/hqk,khd->hqd/dot_general | solution.py:79
  400.2 12.3 %conditional.2 = ((f32[16,256]{1,0:T(8,128)S(1)}, f32[16,256]{1,0:T(8,128)S(1)}, f32[16,256,64]{1,2,0:T(8,128)})) conditional(s32[]{:T(128)} %convert_element_type.63, (f32[16,256]{1,0:T(8,128)S(1)}, f32[16,256]{1,0:T(8,128)S(1)}, f32[16,256,64]{1,2,0:T(8,128)}) %tuple.46, (bf16[16,2,10,16,2,1024]{5,4,3,2,1,0:T(2,128)(2,1)}, s32[]{:T(128)}, ...), branch_computations={%region_2.2_spmd, %region_3.5_spmd} | conditional | flops 346562560 | bytes 46137424 | solution.py:90
  407.5 4.9 %fusion.7 = f32[16,256,64]{1,2,0:T(8,128)} fusion(f32[16,320,256]{2,1,0:T(8,128)} %copy-done.2, f32[16,256]{1,0:T(8,128)S(1)} %max.3, bf16[320,16,64]{2,1,0:T(8,128)(2,1)S(1)} %squeeze.25, f32[16,256,64]{1,2,0:T(8,128)} %get-tuple-element.163, f32[16,256]{1,0:T(8,128)S(1)} %get-tuple-element.243), kind=kOutput, calls=%fused_computation.8 | convolution fusion | flops 172228608 | bytes 8028160 | tf_op jit(solution)/shard_map/while/body/eval_jaxpr/cond/branch_1_fun/hqk,khd->hqd/dot_general | solution.py:79
  414.8 12.3 %conditional.2 = ((f32[16,256]{1,0:T(8,128)S(1)}, f32[16,256]{1,0:T(8,128)S(1)}, f32[16,256,64]{1,2,0:T(8,128)})) conditional(s32[]{:T(128)} %convert_element_type.63, (f32[16,256]{1,0:T(8,128)S(1)}, f32[16,256]{1,0:T(8,128)S(1)}, f32[16,256,64]{1,2,0:T(8,128)}) %tuple.46, (bf16[16,2,10,16,2,1024]{5,4,3,2,1,0:T(2,128)(2,1)}, s32[]{:T(128)}, ...), branch_computations={%region_2.2_spmd, %region_3.5_spmd} | conditional | flops 346562560 | bytes 46137424 | solution.py:90
  422.2 4.9 %fusion.7 = f32[16,256,64]{1,2,0:T(8,128)} fusion(f32[16,320,256]{2,1,0:T(8,128)} %copy-done.2, f32[16,256]{1,0:T(8,128)S(1)} %max.3, bf16[320,16,64]{2,1,0:T(8,128)(2,1)S(1)} %squeeze.25, f32[16,256,64]{1,2,0:T(8,128)} %get-tuple-element.163, f32[16,256]{1,0:T(8,128)S(1)} %get-tuple-element.243), kind=kOutput, calls=%fused_computation.8 | convolution fusion | flops 172228608 | bytes 8028160 | tf_op jit(solution)/shard_map/while/body/eval_jaxpr/cond/branch_1_fun/hqk,khd->hqd/dot_general | solution.py:79
  429.4 12.3 %conditional.2 = ((f32[16,256]{1,0:T(8,128)S(1)}, f32[16,256]{1,0:T(8,128)S(1)}, f32[16,256,64]{1,2,0:T(8,128)})) conditional(s32[]{:T(128)} %convert_element_type.63, (f32[16,256]{1,0:T(8,128)S(1)}, f32[16,256]{1,0:T(8,128)S(1)}, f32[16,256,64]{1,2,0:T(8,128)}) %tuple.46, (bf16[16,2,10,16,2,1024]{5,4,3,2,1,0:T(2,128)(2,1)}, s32[]{:T(128)}, ...), branch_computations={%region_2.2_spmd, %region_3.5_spmd} | conditional | flops 346562560 | bytes 46137424 | solution.py:90
  436.8 4.9 %fusion.7 = f32[16,256,64]{1,2,0:T(8,128)} fusion(f32[16,320,256]{2,1,0:T(8,128)} %copy-done.2, f32[16,256]{1,0:T(8,128)S(1)} %max.3, bf16[320,16,64]{2,1,0:T(8,128)(2,1)S(1)} %squeeze.25, f32[16,256,64]{1,2,0:T(8,128)} %get-tuple-element.163, f32[16,256]{1,0:T(8,128)S(1)} %get-tuple-element.243), kind=kOutput, calls=%fused_computation.8 | convolution fusion | flops 172228608 | bytes 8028160 | tf_op jit(solution)/shard_map/while/body/eval_jaxpr/cond/branch_1_fun/hqk,khd->hqd/dot_general | solution.py:79
  (228 shorter events, 173.4 us)
Async XLA Ops:
  6.5 4.6 %copy-start = (bf16[1024,1024]{1,0:T(8,128)(2,1)S(1)}, bf16[1024,1024]{1,0:T(8,128)(2,1)}, u32[]{:S(2)}) copy-start(bf16[1024,1024]{1,0:T(8,128)(2,1)} %param.15) | copy-start | bytes 6291460
  6.5 161.3 %all-gather.2.cloned.1.call-start = ((), (), s32[]{:S(2)}) async-start(), calls=%async_computation | async-start | bytes 22282240 | tf_op jit(solution)/shard_map/all_gather | solution.py:98
  14.9 12.6 %collective-permute-start = (bf16[2,2,16,2,1024]{4,2,3,1,0:T(8,128)(2,1)S(1)}, bf16[2,2,16,2,1024]{4,2,3,1,0:T(8,128)(2,1)S(1)}, u32[]{:S(2)}, u32[]{:S(2)}) collective-permute-start(bf16[2,2,16,2,1024]{4,2,3,1,0:T(8,128)(2,1)S(1)} %pad_maximum_fusion.1), channel_id=1, source_target_pairs={{0,8},{1,9},{2,10},{3,11},{4,12},{5,13},{6,14},{7,15},{8,0},{9,1},... | collective-permute-start | bytes 786440 | tf_op jit(solution)/shard_map/ppermute | solution.py:25
  18.6 7.8 %collective-permute-start.1 = (bf16[2,1,16,2,1024]{4,2,3,1,0:T(8,128)(2,1)S(1)}, bf16[2,1,16,2,1024]{4,2,3,1,0:T(8,128)(2,1)S(1)}, u32[]{:S(2)}, u32[]{:S(2)}) collective-permute-start(bf16[2,1,16,2,1024]{4,2,3,1,0:T(8,128)(2,1)S(1)} %get-tuple-element.248), channel_id=1, source_target_pairs={{0,16},{16,32},{32,48},{48,64},{64,80},{80,96},{96,112},{112,128},... | collective-permute-start | bytes 393224 | tf_op jit(solution)/shard_map/ppermute | solution.py:16
  20.8 6.8 %collective-permute-start.2 = (bf16[2,1,16,2,1024]{4,2,3,1,0:T(8,128)(2,1)S(1)}, bf16[2,1,16,2,1024]{4,2,3,1,0:T(8,128)(2,1)S(1)}, u32[]{:S(2)}, u32[]{:S(2)}) collective-permute-start(bf16[2,1,16,2,1024]{4,2,3,1,0:T(8,128)(2,1)S(1)} %get-tuple-element.249), channel_id=1, source_target_pairs={{16,0},{32,16},{48,32},{64,48},{80,64},{96,80},{112,96},{128,112},... | collective-permute-start | bytes 393224 | tf_op jit(solution)/shard_map/ppermute | solution.py:17
  27.6 1.3 copy-start.3
  28.8 1.2 copy-start.5
  28.8 1.8 copy-start.6
  214.0 2.3 copy-start.2
  228.7 2.3 copy-start.2
  243.3 2.3 copy-start.2
  258.0 2.3 copy-start.2
  272.6 2.3 copy-start.2
  287.2 2.3 copy-start.2
  301.9 2.3 copy-start.2
  316.5 2.3 copy-start.2
  331.2 2.3 copy-start.2
  345.8 2.3 copy-start.2
  360.5 2.3 copy-start.2
  375.1 2.3 copy-start.2
  389.8 2.3 copy-start.2
  404.4 2.3 copy-start.2
  419.0 2.3 copy-start.2
  433.7 2.3 copy-start.2
  441.7 1.5 copy-start.4
  443.2 3.6 copy-start.1
Sparse Core Ops, SparseCore 0:
  29.0 138.8 all-gather.1
where the time goes:
time: 455 us; the launch traced here: 454 us
  local copies, waits for them, and re-layouts  142 us (31%)
  waiting for transfers between devices  139 us (31%)
  matrix products  99.8 us (22%)
  loops' own time  30 us (7%)
  other arithmetic  21.2 us (5%)
  between operations  13.6 us (3%)
  starting transfers between devices  7.33 us (2%)
    all_gather x1, waiting for transfers between devices, body(): piece = lax.all_gather(extended, 'lon', axis=2, tiled=True)  134 us
    dot_general x16, matrix products, update(): jnp.einsum('hqk,khd->hqd', raw.astype(jnp.bfloat16), value_heads, preferr...  78.7 us
    slice x16, local copies, waits for them, and re-layouts, update(): value_heads = piece[1].reshape(-1, heads, HD)  41.9 us
    while x1, local copies, waits for them, and re-layouts, body(): lax.scan(advance, carry, (split, jnp.arange(count, dtype=jnp.int32)))  38.5 us
    another operation x1, loops' own time, body(): lax.scan(advance, carry, (split, jnp.arange(count, dtype=jnp.int32)))  28.8 us
    cond x48, local copies, waits for them, and re-layouts  23.1 us
    reduce_sum x16, other arithmetic, update(): total = total * fade + jnp.sum(raw, -1)  14.1 us
    dot_general x16, matrix products, update(): jnp.einsum('qhd,khd->hqk', query_heads, key_heads, preferred_element_type...  13.4 us
  transfers between devices with their start and end apart: 4, of which 3 were waited for; matrix products, arithmetic and copies ran while one was open for 1% of the time, Pallas kernels for 0%

commit v1 on v0

v1 whole, which is shorter than its diff:
```python
import functools
import math

import jax
import jax.numpy as jnp
from jax import lax
from jax.experimental import pallas as pl
from jax.experimental.pallas import tpu as pltpu
from jax.sharding import PartitionSpec as P

HD = 64
TOK = 256
EDGE = 32
BLOCKS = 16
OWN = BLOCKS * TOK
HALO = BLOCKS * EDGE
ROWS = 80
QSCALE = HD ** -0.5 * math.log2(math.e)
SAFE = 60.0
NEG = -1e30
PAIR = 2
F32 = jnp.float32
BF16 = jnp.bfloat16
VMEM = pl.BlockSpec(memory_space=pltpu.VMEM)
SMEM = pl.BlockSpec(memory_space=pltpu.SMEM)


def project_kernel(x_ref, gain_ref, wq_ref, wk_ref, wv_ref, out_ref, normed_ref):
    @pl.when(pl.program_id(0) == 0)
    def _():
        wide = x_ref[...].astype(F32)
        mean = jnp.mean(wide * wide, -1, keepdims=True)
        normed_ref[...] = (wide * lax.rsqrt(mean + 1e-06) * gain_ref[...].astype(F32)[None, :]).astype(BF16)

    x = normed_ref[...]
    for slot, (w_ref, scale) in enumerate(((wq_ref, QSCALE), (wk_ref, None), (wv_ref, None))):
        y = jnp.dot(x, w_ref[...], preferred_element_type=F32)
        if scale is not None:
            y = y * scale
        y = y.astype(BF16).T
        for h in range(y.shape[0] // HD):
            out_ref[h, slot * HD : (slot + 1) * HD, :] = y[h * HD : (h + 1) * HD]


def project(x, gain, wq, wk, wv):
    tokens, width = x.shape
    heads = width // HD
    steps = 4
    cols = width // steps
    w_spec = pl.BlockSpec((width, cols), lambda c: (0, c))
    return pl.pallas_call(
        project_kernel,
        grid=(steps,),
        out_shape=jax.ShapeDtypeStruct((heads, 3 * HD, tokens), BF16),
        in_specs=[
            pl.BlockSpec((tokens, width), lambda c: (0, 0)),
            pl.BlockSpec((width,), lambda c: (0,)),
            w_spec,
            w_spec,
            w_spec,
        ],
        out_specs=pl.BlockSpec((heads // steps, 3 * HD, tokens), lambda c: (c, 0, 0)),
        scratch_shapes=[pltpu.VMEM((tokens, width), BF16)],
        name="project",
    )(x, gain, wq, wk, wv)


def edges_kernel(scal_ref, recv_ref, a_ref, b_ref):
    odd = scal_ref[3] == 1
    for j in range(BLOCKS):
        low = recv_ref[j, HD:, 0:128].T[:EDGE]
        high = recv_ref[j, HD:, 128:256].T[128 - EDGE :]
        rows = slice(j * EDGE, (j + 1) * EDGE)
        a_ref[rows, :] = jnp.where(odd, low, high)
        b_ref[rows, :] = jnp.where(odd, high, low)


def edges(scalars, recv):
    shape = jax.ShapeDtypeStruct((HALO, 2 * HD), BF16)
    return pl.pallas_call(
        edges_kernel,
        out_shape=(shape, shape),
        in_specs=[SMEM, VMEM],
        out_specs=[VMEM] * 2,
        compiler_params=pltpu.CompilerParams(vmem_limit_bytes=8 << 20),
        name="edges",
    )(scalars, recv)


def pieces(total, most=1536):
    spans, at = [], 0
    while at < total:
        size = min(most, total - at)
        spans.append((at, size))
        at += size
    return spans


def unit_rows():
    return (lax.broadcasted_iota(jnp.int32, (ROWS - HD, 1), 0) == 0).astype(F32)


def prepare_kernel(scal_ref, recv_ref, k_ref, vt_ref, peak_ref):
    first, final = scal_ref[0] == 0, scal_ref[0] == scal_ref[4]
    lane = lax.broadcasted_iota(jnp.int32, (1, TOK), 1)
    twice = jnp.logical_or(
        jnp.logical_and(first, lane < EDGE), jnp.logical_and(final, lane >= TOK - EDGE)
    )
    times = jnp.where(twice, 2.0, 1.0).astype(F32)
    ones = (unit_rows() * times).astype(BF16)
    q_most = jnp.zeros((1, TOK), F32)
    k_most = jnp.zeros((1, TOK), F32)
    for j in range(BLOCKS):
        q = recv_ref[j, 0:HD, :].astype(F32)
        k = recv_ref[j, HD : 2 * HD, :]
        kf = k.astype(F32)
        q_most = jnp.maximum(q_most, jnp.sum(q * q, 0, keepdims=True))
        k_most = jnp.maximum(k_most, jnp.sum(kf * kf, 0, keepdims=True))
        v = (recv_ref[j, 2 * HD :, :].astype(F32) * times).astype(BF16)
        kt = k.T
        for copy in range(2):
            at = (copy * BLOCKS + j) * TOK
            k_ref[at : at + TOK, :] = kt
            vt_ref[0:HD, at : at + TOK] = v
            vt_ref[HD:, at : at + TOK] = ones
    peak_ref[0, 0] = jnp.max(q_most)
    peak_ref[0, 1] = jnp.max(k_most)


def prepare(scalars, recv):
    return pl.pallas_call(
        prepare_kernel,
        out_shape=(
            jax.ShapeDtypeStruct((2 * OWN, HD), BF16),
            jax.ShapeDtypeStruct((ROWS, 2 * OWN), BF16),
            jax.ShapeDtypeStruct((1, 2), F32),
        ),
        in_specs=[SMEM, VMEM],
        out_specs=[VMEM, VMEM, SMEM],
        compiler_params=pltpu.CompilerParams(vmem_limit_bytes=12 << 20),
        cost_estimate=pl.CostEstimate(flops=10**9, bytes_accessed=6 << 20, transcendentals=0),
        name="prepare",
    )(scalars, recv)


def attend_kernel(scal_ref, peak_ref, recv_ref, k_ref, vt_ref, a_ref, b_ref, out_ref, hk_ref, hvt_ref):
    band, start, width = scal_ref[0], scal_ref[1], scal_ref[2]
    polar = jnp.logical_or(band == 0, band == scal_ref[4])
    k_peak = peak_ref[0, 1]
    for n, ref in enumerate((a_ref, b_ref)):
        rows = slice(n * HALO, (n + 1) * HALO)
        kv = ref[...]
        kf = kv[:, 0:HD].astype(F32)
        k_peak = jnp.maximum(k_peak, jnp.max(jnp.sum(kf * kf, 1, keepdims=True)))
        hk_ref[rows, :] = kv[:, 0:HD]
        hvt_ref[0:HD, rows] = kv.T[HD:]
        hvt_ref[HD:, rows] = jnp.broadcast_to(unit_rows(), (ROWS - HD, HALO)).astype(BF16)
    safe = peak_ref[0, 0] * k_peak < SAFE * SAFE

    def plain(acc, qt, keys, values, seen=None):
        s = jnp.dot(keys, qt, preferred_element_type=F32)
        p = jnp.exp2(s).astype(BF16)
        if seen is not None:
            values = jnp.where(seen, values.astype(F32), 0.0).astype(BF16)
        return acc + jnp.dot(values, p, preferred_element_type=F32)

    def shifted(state, qt, keys, values, seen=None):
        top, acc = state
        s = jnp.dot(keys, qt, preferred_element_type=F32)
        if seen is not None:
            s = jnp.where(seen, s, NEG)
        new = jnp.maximum(top, jnp.max(s, 0, keepdims=True))
        raw = jnp.exp2(s - new)
        if seen is not None:
            raw = jnp.where(seen, raw, 0.0)
        fresh = jnp.dot(values, raw.astype(BF16), preferred_element_type=F32)
        return new, acc * jnp.exp2(top - new) + fresh

    def own(at, size):
        return k_ref[pl.ds(at, size), :], vt_ref[:, pl.ds(at, size)]

    def halo(at, size):
        return hk_ref[pl.ds(at, size), :], hvt_ref[:, pl.ds(at, size)]

    def finish(j, acc):
        out_ref[j] = (acc[0:HD] / acc[HD : HD + 1]).astype(BF16)

    def base_of(j):
        return jnp.bitwise_and(j + start + BLOCKS, BLOCKS - 1)

    def in_window(edge_key, base):
        block = jnp.bitwise_and(lax.shift_right_logical(edge_key, 5), BLOCKS - 1)
        return jnp.bitwise_and(block - base + BLOCKS, BLOCKS - 1) < width

    zero = jnp.zeros((ROWS, TOK), F32)

    @pl.when(jnp.logical_and(safe, polar))
    def _():
        @pl.loop(0, BLOCKS, step=PAIR)
        def _(first):
            for j in (first + n for n in range(PAIR)):
                qt = recv_ref[j, 0:HD, :]
                acc = zero
                for at, size in pieces(OWN):
                    acc = plain(acc, qt, *own(at, size))
                acc = plain(acc, qt, *halo(0, HALO))
                finish(j, acc)

    grain = 4
    for count in range(grain, BLOCKS + 1, grain):
        fits = jnp.logical_and(width <= count, width > count - grain)

        @pl.when(jnp.logical_and(jnp.logical_and(safe, jnp.logical_not(polar)), fits))
        def _(count=count):
            @pl.loop(0, BLOCKS, step=PAIR)
            def _(first):
                for j in (first + n for n in range(PAIR)):
                    qt = recv_ref[j, 0:HD, :]
                    base = base_of(j)
                    acc = zero
                    for at, size in pieces(count * TOK):
                        seen = None
                        if at + size > (count - grain + 1) * TOK:
                            lanes = lax.broadcasted_iota(jnp.int32, (1, size), 1)
                            seen = lanes < width * TOK - at
                        acc = plain(acc, qt, *own(pl.multiple_of(base * TOK + at, TOK), size), seen)
                    lanes = lax.broadcasted_iota(jnp.int32, (1, 2 * HALO), 1)
                    acc = plain(acc, qt, *halo(0, 2 * HALO), in_window(lanes, base))
                    finish(j, acc)

    @pl.when(jnp.logical_not(safe))
    def _():
        @pl.loop(0, BLOCKS)
        def _(j):
            qt = recv_ref[j, 0:HD, :]
            base = base_of(j)

            def own_step(n, state):
                return shifted(state, qt, *own(pl.multiple_of((base + n) * TOK, TOK), TOK))

            def halo_step(n, state):
                at = pl.multiple_of(n * TOK, TOK)
                row = lax.broadcasted_iota(jnp.int32, (TOK, 1), 0) + at
                return shifted(state, qt, *halo(at, TOK), in_window(row, base))

            state = (jnp.full((1, TOK), NEG, F32), zero)
            state = lax.fori_loop(0, width, own_step, state)
            sides = jnp.where(polar, HALO // TOK, 2 * HALO // TOK)
            state = lax.fori_loop(0, sides, halo_step, state)
            finish(j, state[1])


def attend(scalars, peaks, recv, keys, values, side_a, side_b):
    return pl.pallas_call(
        attend_kernel,
        out_shape=jax.ShapeDtypeStruct((BLOCKS, HD, TOK), BF16),
        in_specs=[SMEM, SMEM] + [VMEM] * 5,
        out_specs=VMEM,
        scratch_shapes=[
            pltpu.VMEM((2 * HALO, HD), BF16),
            pltpu.VMEM((ROWS, 2 * HALO), BF16),
        ],
        compiler_params=pltpu.CompilerParams(vmem_limit_bytes=24 << 20),
        cost_estimate=pl.CostEstimate(
            flops=4 * OWN * OWN * HD, bytes_accessed=8 << 20, transcendentals=OWN * OWN
        ),
        name="attend",
    )(scalars, peaks, recv, keys, values, side_a, side_b)


def mix_kernel(att_ref, wo_ref, x_ref, out_ref, rows_ref):
    @pl.when(pl.program_id(0) == 0)
    def _():
        rows_ref[...] = att_ref[...].T

    y = jnp.dot(rows_ref[...], wo_ref[...], preferred_element_type=F32)
    out_ref[...] = (x_ref[...].astype(F32) + y).astype(BF16)


def mix(att, wo, x):
    tokens, width = x.shape
    steps = 4
    cols = width // steps
    return pl.pallas_call(
        mix_kernel,
        grid=(steps,),
        out_shape=jax.ShapeDtypeStruct((tokens, width), BF16),
        in_specs=[
            pl.BlockSpec((width, tokens), lambda c: (0, 0)),
            pl.BlockSpec((width, cols), lambda c: (0, c)),
            pl.BlockSpec((tokens, cols), lambda c: (0, c)),
        ],
        out_specs=pl.BlockSpec((tokens, cols), lambda c: (0, c)),
        scratch_shapes=[pltpu.VMEM((tokens, width), BF16)],
        name="mix",
    )(att, wo, x)


def swap(value):
    return lax.all_to_all(value, "lon", split_axis=0, concat_axis=0, tiled=True)


def body(tokens, norm_gain, q_weight, k_weight, v_weight, o_weight, band_start, band_width):
    width = tokens.shape[-1]
    n_lat = lax.axis_size("lat")
    band = lax.axis_index("lat")
    scalars = jnp.stack(
        [band, band_start[band], band_width[band], jnp.bitwise_and(band, 1), jnp.int32(n_lat - 1)]
    )
    x = tokens.reshape(-1, width)
    recv = swap(project(x, norm_gain, q_weight, k_weight, v_weight))
    side_a, side_b = edges(scalars, recv)
    pairs_a = [(b, b ^ 1) for b in range(n_lat)]
    pairs_b = [(b, ((b - 1) ^ 1) + 1) for b in range(1, n_lat - 1)]
    side_a = lax.ppermute(side_a, "lat", pairs_a)
    side_b = lax.ppermute(side_b, "lat", pairs_b)
    keys, values, peaks = prepare(scalars, recv)
    att = swap(attend(scalars, peaks, recv, keys, values, side_a, side_b))
    mixed = mix(att.reshape(width, -1), o_weight, x)
    return mixed.reshape(tokens.shape)


def solution(mesh):
    placed = (P("lat", "lon", None, None), P(), P(), P(), P(), P(), P(), P())
    return jax.shard_map(
        body, mesh=mesh, in_specs=placed, out_specs=P("lat", "lon", None, None), check_vma=False
    )
```

time: 455 us -> 184 us (0.40)
  local copies, waits for them, and re-layouts: 142 us -> 6.8 us
  Pallas kernels: 0 us -> 128 us
  waiting for transfers between devices: 139 us -> 21.3 us
  matrix products: 99.8 us -> 0 us
  loops' own time: 30 us -> 0 us
  other arithmetic: 21.2 us -> 0 us
  blocking collectives: 0 us -> 17.9 us
  between operations: 13.6 us -> 0.04 us
    all_gather x1 -> x0, waiting for transfers between devices: 134 us -> none  [body(): piece = lax.all_gather(extended, 'lon', axis=2, tiled=True)]
    pallas_call x0 -> x5, Pallas kernels: none -> 128 us  [the longest x1 115 us: attend(): pl.pallas_call(attend_kernel, out_shape=jax.ShapeDtypeStruct((BLOCKS, HD,...]
    dot_general x36 -> x0, matrix products: 99.8 us -> none  [the longest x16 78.7 us: update(): jnp.einsum('hqk,khd->hqd', raw.astype(jnp.bfloat16), value_heads, preferr...]
    slice x17 -> x0, local copies, waits for them, and re-layouts: 41.9 us -> none  [the longest x16 41.9 us: update(): value_heads = piece[1].reshape(-1, heads, HD)]
    while x1 -> x0, local copies, waits for them, and re-layouts: 38.5 us -> none  [body(): lax.scan(advance, carry, (split, jnp.arange(count, dtype=jnp.int32)))]
    another operation x17 -> x0, loops' own time: 30 us -> none  [the longest x1 28.8 us: body(): lax.scan(advance, carry, (split, jnp.arange(count, dtype=jnp.int32)))]
    squeeze x32 -> x0, local copies, waits for them, and re-layouts: 24.1 us -> none  [the longest x16 12.1 us: update(): key_heads = piece[0].reshape(-1, heads, HD)]
    cond x48 -> x0, local copies, waits for them, and re-layouts: 23.1 us -> none
  transfers between devices with their start and end apart: 4 -> 3, of which waited for: 3 -> 2; matrix products, arithmetic and copies ran while one was open for 1% -> 1% of each run, Pallas kernels for 0% -> 1%
where the time goes in v1:
time: 184 us
  Pallas kernels  128 us (70%)
  waiting for transfers between devices  21.3 us (12%)
  blocking collectives  17.9 us (10%)
  starting transfers between devices  9.63 us (5%)
  local copies, waits for them, and re-layouts  6.8 us (4%)
    pallas_call x1, Pallas kernels, attend(): pl.pallas_call(attend_kernel, out_shape=jax.ShapeDtypeStruct((BLOCKS, HD,...  115 us
    all_to_all x1, waiting for transfers between devices, swap(): return lax.all_to_all(value, 'lon', split_axis=0, concat_axis=0, tiled=True)  20 us
    all_to_all x1, blocking collectives, swap(): return lax.all_to_all(value, 'lon', split_axis=0, concat_axis=0, tiled=True)  17.9 us
    all_to_all x1, starting transfers between devices, swap(): return lax.all_to_all(value, 'lon', split_axis=0, concat_axis=0, tiled=True)  8.57 us
    pallas_call x1, Pallas kernels, project(): pl.pallas_call(project_kernel, grid=(steps,), out_shape=jax.ShapeDtypeStr...  6.31 us
    pallas_call x1, Pallas kernels, mix(): pl.pallas_call(mix_kernel, grid=(steps,), out_shape=jax.ShapeDtypeStruct(...  4.67 us
  transfers between devices with their start and end apart: 3, of which 2 were waited for; matrix products, arithmetic and copies ran while one was open for 1% of the time, Pallas kernels for 1%

profile of v1, /device:TPU:1, one launch (start us, length us, event | category | flops | bytes accessed | tf_op | source)
XLA Modules:
  0.0 183.8 jit_solution(2057354236119027048)
XLA Ops:
  0.0 2.0 %reshape.9.x_ref = bf16[256,1024]{1,0:T(8,128)(2,1)} reshape(bf16[8,16,2,1024]{3,2,1,0:T(2,128)(2,1)} %param.8) | data formatting | bytes 1048576 | tf_op jit(solution)/shard_map/reshape | solution.py:310
  2.0 6.3 %project.1 = bf16[16,192,256]{2,1,0:T(8,128)(2,1)} custom-call(bf16[256,1024]{1,0:T(8,128)(2,1)} %reshape.9.x_ref, bf16[1024]{0:T(1024)(128)(2,1)} %gain_ref.1, bf16[1024,1024]{1,0:T(8,128)(2,1)} %wq_ref.1, bf16[1024,1024]{1,0:T(8,128)(2,1)} %wk_ref.1, bf16[1024,1024]{1,0:T(8,128)(2,1)} %wv_ref.1), custom_call_target="tpu_custom_call" | custom-call | tf_op jit(solution)/shard_map/project/pallas_call | solution.py:51
  8.3 0.0 copy-start
  8.3 0.0 copy-start.1
  8.3 8.6 %all-to-all-start = ((bf16[16,192,256]{2,1,0:T(8,128)(2,1)}), bf16[16,192,256]{2,1,0:T(8,128)(2,1)S(1)}, u32[]{:S(2)}, u32[]{:S(2)}) async-start(bf16[16,192,256]{2,1,0:T(8,128)(2,1)} %project.1), calls=%async_computation | async-start | bytes 3145728 | tf_op jit(solution)/shard_map/all_to_all | solution.py:300
  16.9 0.0 copy-done
  16.9 0.7 dynamic_slice.7
  17.6 0.0 copy-done.1
  17.6 0.6 dynamic_slice.6
  18.2 1.4 stack.11.scal_ref
  19.7 20.0 %all-to-all-done.recv_ref = bf16[16,192,256]{2,1,0:T(8,128)(2,1)S(1)} async-done(((bf16[16,192,256]{2,1,0:T(8,128)(2,1)}), bf16[16,192,256]{2,1,0:T(8,128)(2,1)S(1)}, u32[]{:S(2)}, u32[]{:S(2)}) %all-to-all-start) | async-done | bytes 1572896 | tf_op jit(solution)/shard_map/all_to_all | solution.py:300
  39.6 0.9 edges.1
  40.5 0.4 collective-permute-start
  40.9 0.7 collective-permute-start.1
  41.6 1.5 prepare.1
  43.1 1.3 collective-permute-done.a_ref
  44.4 0.0 collective-permute-done.1.b_ref
  44.4 114.7 %attend.1 = bf16[16,64,256]{2,1,0:T(8,128)(2,1)S(1)} custom-call(s32[5]{0:T(128)S(1)} %stack.11.scal_ref, f32[1,2]{1,0:T(1,128)S(1)} %get-tuple-element.10.peak_ref, bf16[16,192,256]{2,1,0:T(8,128)(2,1)S(1)} %all-to-all-done.recv_ref, bf16[8192,64]{1,0:T(8,128)(2,1)S(1)} %get-tuple-element.11.k_ref, bf16[80,8192]{1,0:T(8,128)(2,1)S(1)} %get-tuple-element.12.vt_ref, ...), custom_call_target="tpu_custom_call" | custom-call | flops 4294967296 | bytes 8388608 | tf_op jit(solution)/shard_map/attend/pallas_call | solution.py:254
  159.1 17.9 %all_to_all.10 = bf16[16,64,256]{2,1,0:T(8,128)(2,1)} all-to-all(bf16[16,64,256]{2,1,0:T(8,128)(2,1)S(1)} %attend.1), channel_id=1, replica_groups=mesh['lat'=16,'lon'=16] {'lon'}, dimensions={0} | all-to-all | bytes 1048576 | tf_op jit(solution)/shard_map/all_to_all | solution.py:300
  177.1 4.7 %mix.1 = bf16[256,1024]{1,0:T(8,128)(2,1)} custom-call(bf16[1024,256]{1,0:T(8,128)(2,1)} %bitcast.3, bf16[1024,1024]{1,0:T(8,128)(2,1)} %wo_ref.1, bf16[256,1024]{1,0:T(8,128)(2,1)} %reshape.9.x_ref), custom_call_target="tpu_custom_call" | custom-call | tf_op jit(solution)/shard_map/mix/pallas_call | solution.py:284
  181.7 2.0 %reshape.11 = bf16[8,16,2,1024]{3,2,1,0:T(2,128)(2,1)} reshape(bf16[256,1024]{1,0:T(8,128)(2,1)} %mix.1) | data formatting | bytes 1048576 | tf_op jit(solution)/shard_map/reshape | solution.py:320
Async XLA Ops:
  8.3 8.6 %copy-start = (s32[16]{0:T(128)S(1)}, s32[16]{0:T(128)}, u32[]{:S(2)}) copy-start(s32[16]{0:T(128)} %param.15) | copy-start | bytes 196
  8.3 9.2 %copy-start.1 = (s32[16]{0:T(128)S(1)}, s32[16]{0:T(128)}, u32[]{:S(2)}) copy-start(s32[16]{0:T(128)} %param.14) | copy-start | bytes 196
  8.3 31.3 %all-to-all-start = ((bf16[16,192,256]{2,1,0:T(8,128)(2,1)}), bf16[16,192,256]{2,1,0:T(8,128)(2,1)S(1)}, u32[]{:S(2)}, u32[]{:S(2)}) async-start(bf16[16,192,256]{2,1,0:T(8,128)(2,1)} %project.1), calls=%async_computation | async-start | bytes 3145728 | tf_op jit(solution)/shard_map/all_to_all | solution.py:300
  40.5 3.9 %collective-permute-start = (bf16[512,128]{1,0:T(8,128)(2,1)S(1)}, bf16[512,128]{1,0:T(8,128)(2,1)S(1)}, u32[]{:S(2)}, u32[]{:S(2)}) collective-permute-start(bf16[512,128]{1,0:T(8,128)(2,1)S(1)} %get-tuple-element.13), channel_id=1, source_target_pairs={{0,16},{16,0},{32,48},{48,32},{64,80},{80,64},{96,112},{112,96},{1... | collective-permute-start | bytes 393224 | tf_op jit(solution)/shard_map/ppermute | solution.py:315
  40.9 3.5 %collective-permute-start.1 = (bf16[512,128]{1,0:T(8,128)(2,1)S(1)}, bf16[512,128]{1,0:T(8,128)(2,1)S(1)}, u32[]{:S(2)}, u32[]{:S(2)}) collective-permute-start(bf16[512,128]{1,0:T(8,128)(2,1)S(1)} %get-tuple-element.14), channel_id=1, source_target_pairs={{16,32},{32,16},{48,64},{64,48},{80,96},{96,80},{112,128},{128,112... | collective-permute-start | bytes 393224 | tf_op jit(solution)/shard_map/ppermute | solution.py:316

commit v2 on v1

--- a/solution.py
+++ b/solution.py
@@ -28,7 +28,7 @@
 def project_kernel(x_ref, gain_ref, wq_ref, wk_ref, wv_ref, out_ref, normed_ref):
     @pl.when(pl.program_id(0) == 0)
     def _():
-        wide = x_ref[...].astype(F32)
+        wide = x_ref[...].reshape(normed_ref.shape).astype(F32)
         mean = jnp.mean(wide * wide, -1, keepdims=True)
         normed_ref[...] = (wide * lax.rsqrt(mean + 1e-06) * gain_ref[...].astype(F32)[None, :]).astype(BF16)
 
@@ -43,9 +43,10 @@
 
 
 def project(x, gain, wq, wk, wv):
-    tokens, width = x.shape
+    width = x.shape[-1]
+    tokens = x.size // width
     heads = width // HD
-    steps = 4
+    steps = 2
     cols = width // steps
     w_spec = pl.BlockSpec((width, cols), lambda c: (0, c))
     return pl.pallas_call(
@@ -53,7 +54,7 @@
         grid=(steps,),
         out_shape=jax.ShapeDtypeStruct((heads, 3 * HD, tokens), BF16),
         in_specs=[
-            pl.BlockSpec((tokens, width), lambda c: (0, 0)),
+            pl.BlockSpec(x.shape, lambda c: (0, 0, 0, 0)),
             pl.BlockSpec((width,), lambda c: (0,)),
             w_spec,
             w_spec,
@@ -268,30 +269,24 @@
     )(scalars, peaks, recv, keys, values, side_a, side_b)
 
 
-def mix_kernel(att_ref, wo_ref, x_ref, out_ref, rows_ref):
-    @pl.when(pl.program_id(0) == 0)
-    def _():
-        rows_ref[...] = att_ref[...].T
-
-    y = jnp.dot(rows_ref[...], wo_ref[...], preferred_element_type=F32)
-    out_ref[...] = (x_ref[...].astype(F32) + y).astype(BF16)
+def mix_kernel(att_ref, wo_ref, x_ref, out_ref):
+    rows = att_ref[...].T
+    width = wo_ref.shape[1]
+    cols = width // 2
+    for at in range(0, width, cols):
+        part = slice(at, at + cols)
+        y = jnp.dot(rows, wo_ref[:, part], preferred_element_type=F32)
+        y = y + x_ref[:, :, :, part].reshape(y.shape).astype(F32)
+        out_ref[:, :, :, part] = y.astype(BF16).reshape(out_ref.shape[:3] + (cols,))
 
 
 def mix(att, wo, x):
-    tokens, width = x.shape
-    steps = 4
-    cols = width // steps
     return pl.pallas_call(
         mix_kernel,
-        grid=(steps,),
-        out_shape=jax.ShapeDtypeStruct((tokens, width), BF16),
-        in_specs=[
-            pl.BlockSpec((width, tokens), lambda c: (0, 0)),
-            pl.BlockSpec((width, cols), lambda c: (0, c)),
-            pl.BlockSpec((tokens, cols), lambda c: (0, c)),
-        ],
-        out_specs=pl.BlockSpec((tokens, cols), lambda c: (0, c)),
-        scratch_shapes=[pltpu.VMEM((tokens, width), BF16)],
+        out_shape=jax.ShapeDtypeStruct(x.shape, BF16),
+        in_specs=[VMEM] * 3,
+        out_specs=VMEM,
+        compiler_params=pltpu.CompilerParams(vmem_limit_bytes=10 << 20),
         name="mix",
     )(att, wo, x)
 
@@ -307,8 +302,7 @@
     scalars = jnp.stack(
         [band, band_start[band], band_width[band], jnp.bitwise_and(band, 1), jnp.int32(n_lat - 1)]
     )
-    x = tokens.reshape(-1, width)
-    recv = swap(project(x, norm_gain, q_weight, k_weight, v_weight))
+    recv = swap(project(tokens, norm_gain, q_weight, k_weight, v_weight))
     side_a, side_b = edges(scalars, recv)
     pairs_a = [(b, b ^ 1) for b in range(n_lat)]
     pairs_b = [(b, ((b - 1) ^ 1) + 1) for b in range(1, n_lat - 1)]
@@ -316,8 +310,7 @@
     side_b = lax.ppermute(side_b, "lat", pairs_b)
     keys, values, peaks = prepare(scalars, recv)
     att = swap(attend(scalars, peaks, recv, keys, values, side_a, side_b))
-    mixed = mix(att.reshape(width, -1), o_weight, x)
-    return mixed.reshape(tokens.shape)
+    return mix(att.reshape(width, -1), o_weight, tokens)
 
 
 def solution(mesh):

time: 184 us -> 176 us (0.957)
  local copies, waits for them, and re-layouts: 6.8 us -> 2.53 us
  Pallas kernels: 128 us -> 125 us
    reshape x2 -> x0, local copies, waits for them, and re-layouts: 4.07 us -> none  [the longest x1 2.03 us: body(): x = tokens.reshape(-1, width)]
    pallas_call x1, Pallas kernels: 4.67 us -> 1.61 us  [mix(): pl.pallas_call(mix_kernel, out_shape=jax.ShapeDtypeStruct(x.shape, BF16),...]
where the time goes in v2:
time: 176 us
  Pallas kernels  125 us (71%)
  waiting for transfers between devices  21.5 us (12%)
  blocking collectives  17.8 us (10%)
  starting transfers between devices  9.63 us (5%)
  local copies, waits for them, and re-layouts  2.53 us (1%)
    pallas_call x1, Pallas kernels, attend(): pl.pallas_call(attend_kernel, out_shape=jax.ShapeDtypeStruct((BLOCKS, HD,...  115 us
    all_to_all x1, waiting for transfers between devices, swap(): return lax.all_to_all(value, 'lon', split_axis=0, concat_axis=0, tiled=True)  20.2 us
    all_to_all x1, blocking collectives, swap(): return lax.all_to_all(value, 'lon', split_axis=0, concat_axis=0, tiled=True)  17.8 us
    all_to_all x1, starting transfers between devices, swap(): return lax.all_to_all(value, 'lon', split_axis=0, concat_axis=0, tiled=True)  8.57 us
    pallas_call x1, Pallas kernels, project(): pl.pallas_call(project_kernel, grid=(steps,), out_shape=jax.ShapeDtypeStr...  5.8 us
  transfers between devices with their start and end apart: 3, of which 2 were waited for; matrix products, arithmetic and copies ran while one was open for 1% of the time, Pallas kernels for 1%

profile of v2, /device:TPU:1, one launch (start us, length us, event | category | flops | bytes accessed | tf_op | source)
XLA Modules:
  0.0 176.0 jit_solution(12453761631592077799)
XLA Ops:
  0.0 5.8 %project.1 = bf16[16,192,256]{2,1,0:T(8,128)(2,1)} custom-call(bf16[8,16,2,1024]{3,2,1,0:T(2,128)(2,1)} %x_ref.3, bf16[1024]{0:T(1024)(128)(2,1)} %gain_ref.1, bf16[1024,1024]{1,0:T(8,128)(2,1)} %wq_ref.1, bf16[1024,1024]{1,0:T(8,128)(2,1)} %wk_ref.1, bf16[1024,1024]{1,0:T(8,128)(2,1)} %wv_ref.1), custom_call_target="tpu_custom_call" | custom-call | tf_op jit(solution)/shard_map/project/pallas_call | solution.py:52
  5.8 0.0 copy-start.2
  5.8 0.0 copy-start.3
  5.8 8.6 %all-to-all-start = ((bf16[16,192,256]{2,1,0:T(8,128)(2,1)}), bf16[16,192,256]{2,1,0:T(8,128)(2,1)S(1)}, u32[]{:S(2)}, u32[]{:S(2)}) async-start(bf16[16,192,256]{2,1,0:T(8,128)(2,1)} %project.1), calls=%async_computation | async-start | bytes 3145728 | tf_op jit(solution)/shard_map/all_to_all | solution.py:295
  14.4 0.0 copy-done.2
  14.4 0.6 dynamic_slice.7
  15.0 0.0 copy-done.3
  15.0 0.6 dynamic_slice.6
  15.6 1.3 stack.11.scal_ref
  16.9 20.2 %all-to-all-done.recv_ref = bf16[16,192,256]{2,1,0:T(8,128)(2,1)S(1)} async-done(((bf16[16,192,256]{2,1,0:T(8,128)(2,1)}), bf16[16,192,256]{2,1,0:T(8,128)(2,1)S(1)}, u32[]{:S(2)}, u32[]{:S(2)}) %all-to-all-start) | async-done | bytes 1572896 | tf_op jit(solution)/shard_map/all_to_all | solution.py:295
  37.1 0.9 edges.1
  38.0 0.4 collective-permute-start
  38.4 0.7 collective-permute-start.1
  39.0 1.5 prepare.1
  40.6 1.3 collective-permute-done.a_ref
  41.9 0.0 collective-permute-done.1.b_ref
  41.9 0.0 copy-start
  41.9 0.0 copy-start.1
  41.9 114.7 %attend.1 = bf16[16,64,256]{2,1,0:T(8,128)(2,1)S(1)} custom-call(s32[5]{0:T(128)S(1)} %stack.11.scal_ref, f32[1,2]{1,0:T(1,128)S(1)} %get-tuple-element.10.peak_ref, bf16[16,192,256]{2,1,0:T(8,128)(2,1)S(1)} %all-to-all-done.recv_ref, bf16[8192,64]{1,0:T(8,128)(2,1)S(1)} %get-tuple-element.11.k_ref, bf16[80,8192]{1,0:T(8,128)(2,1)S(1)} %get-tuple-element.12.vt_ref, ...), custom_call_target="tpu_custom_call" | custom-call | flops 4294967296 | bytes 8388608 | tf_op jit(solution)/shard_map/attend/pallas_call | solution.py:255
  156.6 17.8 %all_to_all.10 = bf16[16,64,256]{2,1,0:T(8,128)(2,1)S(1)} all-to-all(bf16[16,64,256]{2,1,0:T(8,128)(2,1)S(1)} %attend.1), channel_id=1, replica_groups=mesh['lat'=16,'lon'=16] {'lon'}, dimensions={0} | all-to-all | bytes 1048576 | tf_op jit(solution)/shard_map/all_to_all | solution.py:295
  174.4 0.0 copy-done
  174.4 0.0 copy-done.1
  174.4 1.6 mix.1
Async XLA Ops:
  5.8 8.6 %copy-start.2 = (s32[16]{0:T(128)S(1)}, s32[16]{0:T(128)}, u32[]{:S(2)}) copy-start(s32[16]{0:T(128)} %param.15) | copy-start | bytes 196
  5.8 9.1 %copy-start.3 = (s32[16]{0:T(128)S(1)}, s32[16]{0:T(128)}, u32[]{:S(2)}) copy-start(s32[16]{0:T(128)} %param.14) | copy-start | bytes 196
  5.8 31.3 %all-to-all-start = ((bf16[16,192,256]{2,1,0:T(8,128)(2,1)}), bf16[16,192,256]{2,1,0:T(8,128)(2,1)S(1)}, u32[]{:S(2)}, u32[]{:S(2)}) async-start(bf16[16,192,256]{2,1,0:T(8,128)(2,1)} %project.1), calls=%async_computation | async-start | bytes 3145728 | tf_op jit(solution)/shard_map/all_to_all | solution.py:295
  38.0 3.9 %collective-permute-start = (bf16[512,128]{1,0:T(8,128)(2,1)S(1)}, bf16[512,128]{1,0:T(8,128)(2,1)S(1)}, u32[]{:S(2)}, u32[]{:S(2)}) collective-permute-start(bf16[512,128]{1,0:T(8,128)(2,1)S(1)} %get-tuple-element.13), channel_id=1, source_target_pairs={{0,16},{16,0},{32,48},{48,32},{64,80},{80,64},{96,112},{112,96},{1... | collective-permute-start | bytes 393224 | tf_op jit(solution)/shard_map/ppermute | solution.py:309
  38.4 3.5 %collective-permute-start.1 = (bf16[512,128]{1,0:T(8,128)(2,1)S(1)}, bf16[512,128]{1,0:T(8,128)(2,1)S(1)}, u32[]{:S(2)}, u32[]{:S(2)}) collective-permute-start(bf16[512,128]{1,0:T(8,128)(2,1)S(1)} %get-tuple-element.14), channel_id=1, source_target_pairs={{16,32},{32,16},{48,64},{64,48},{80,96},{96,80},{112,128},{128,112... | collective-permute-start | bytes 393224 | tf_op jit(solution)/shard_map/ppermute | solution.py:310
  41.9 132.5 %copy-start = (bf16[8,16,2,1024]{3,2,1,0:T(2,128)(2,1)S(1)}, bf16[8,16,2,1024]{3,2,1,0:T(2,128)(2,1)}, u32[]{:S(2)}) copy-start(bf16[8,16,2,1024]{3,2,1,0:T(2,128)(2,1)} %x_ref.3) | copy-start | bytes 1572868
  41.9 132.5 %copy-start.1 = (bf16[1024,1024]{1,0:T(8,128)(2,1)S(1)}, bf16[1024,1024]{1,0:T(8,128)(2,1)}, u32[]{:S(2)}) copy-start(bf16[1024,1024]{1,0:T(8,128)(2,1)} %wo_ref.1) | copy-start | bytes 6291460

commit v3 on v2

--- a/solution.py
+++ b/solution.py
@@ -19,6 +19,8 @@
 SAFE = 60.0
 NEG = -1e30
 PAIR = 2
+PRE = 2
+GRAIN = 4
 F32 = jnp.float32
 BF16 = jnp.bfloat16
 VMEM = pl.BlockSpec(memory_space=pltpu.VMEM)
@@ -97,11 +99,45 @@
     return spans
 
 
+def variants(width, polar):
+    yield None, polar
+    for count in range(GRAIN, BLOCKS + 1, GRAIN):
+        fits = jnp.logical_and(width <= count, width > count - GRAIN)
+        yield count, jnp.logical_and(jnp.logical_not(polar), fits)
+
+
 def unit_rows():
     return (lax.broadcasted_iota(jnp.int32, (ROWS - HD, 1), 0) == 0).astype(F32)
 
 
-def prepare_kernel(scal_ref, recv_ref, k_ref, vt_ref, peak_ref):
+def plain(acc, qt, keys, values, seen=None):
+    s = jnp.dot(keys, qt, preferred_element_type=F32)
+    p = jnp.exp2(s).astype(BF16)
+    if seen is not None:
+        values = jnp.where(seen, values.astype(F32), 0.0).astype(BF16)
+    return acc + jnp.dot(values, p, preferred_element_type=F32)
+
+
+def window_base(j, start):
+    return jnp.bitwise_and(j + start + BLOCKS, BLOCKS - 1)
+
+
+def own_part(qt, base, width, count, k_ref, vt_ref):
+    acc = jnp.zeros((ROWS, TOK), F32)
+    for at, size in pieces(count * TOK):
+        if base is None:
+            place, seen = at, None
+        else:
+            place = pl.multiple_of(base * TOK + at, TOK)
+            seen = None
+            if at + size > (count - GRAIN + 1) * TOK:
+                seen = lax.broadcasted_iota(jnp.int32, (1, size), 1) < width * TOK - at
+        acc = plain(acc, qt, k_ref[pl.ds(place, size), :], vt_ref[:, pl.ds(place, size)], seen)
+    return acc
+
+
+def prepare_kernel(scal_ref, recv_ref, k_ref, vt_ref, peak_ref, acc_ref):
+    start, width = scal_ref[1], scal_ref[2]
     first, final = scal_ref[0] == 0, scal_ref[0] == scal_ref[4]
     lane = lax.broadcasted_iota(jnp.int32, (1, TOK), 1)
     twice = jnp.logical_or(
@@ -124,8 +160,19 @@
             k_ref[at : at + TOK, :] = kt
             vt_ref[0:HD, at : at + TOK] = v
             vt_ref[HD:, at : at + TOK] = ones
-    peak_ref[0, 0] = jnp.max(q_most)
-    peak_ref[0, 1] = jnp.max(k_most)
+    q_peak = jnp.max(q_most)
+    k_peak = jnp.max(k_most)
+    peak_ref[0, 0] = q_peak
+    peak_ref[0, 1] = k_peak
+    safe = q_peak * k_peak < SAFE * SAFE
+    for count, fits in variants(width, jnp.logical_or(first, final)):
+
+        @pl.when(jnp.logical_and(safe, fits))
+        def _(count=count):
+            for j in range(PRE):
+                base = None if count is None else window_base(j, start)
+                qt = recv_ref[j, 0:HD, :]
+                acc_ref[j] = own_part(qt, base, width, count or BLOCKS, k_ref, vt_ref)
 
 
 def prepare(scalars, recv):
@@ -135,16 +182,17 @@
             jax.ShapeDtypeStruct((2 * OWN, HD), BF16),
             jax.ShapeDtypeStruct((ROWS, 2 * OWN), BF16),
             jax.ShapeDtypeStruct((1, 2), F32),
+            jax.ShapeDtypeStruct((PRE, ROWS, TOK), F32),
         ),
         in_specs=[SMEM, VMEM],
-        out_specs=[VMEM, VMEM, SMEM],
-        compiler_params=pltpu.CompilerParams(vmem_limit_bytes=12 << 20),
+        out_specs=[VMEM, VMEM, SMEM, VMEM],
+        compiler_params=pltpu.CompilerParams(vmem_limit_bytes=16 << 20),
         cost_estimate=pl.CostEstimate(flops=10**9, bytes_accessed=6 << 20, transcendentals=0),
         name="prepare",
     )(scalars, recv)
 
 
-def attend_kernel(scal_ref, peak_ref, recv_ref, k_ref, vt_ref, a_ref, b_ref, out_ref, hk_ref, hvt_ref):
+def attend_kernel(scal_ref, peak_ref, recv_ref, k_ref, vt_ref, pre_ref, a_ref, b_ref, out_ref, hk_ref, hvt_ref):
     band, start, width = scal_ref[0], scal_ref[1], scal_ref[2]
     polar = jnp.logical_or(band == 0, band == scal_ref[4])
     k_peak = peak_ref[0, 1]
@@ -158,13 +206,6 @@
         hvt_ref[HD:, rows] = jnp.broadcast_to(unit_rows(), (ROWS - HD, HALO)).astype(BF16)
     safe = peak_ref[0, 0] * k_peak < SAFE * SAFE
 
-    def plain(acc, qt, keys, values, seen=None):
-        s = jnp.dot(keys, qt, preferred_element_type=F32)
-        p = jnp.exp2(s).astype(BF16)
-        if seen is not None:
-            values = jnp.where(seen, values.astype(F32), 0.0).astype(BF16)
-        return acc + jnp.dot(values, p, preferred_element_type=F32)
-
     def shifted(state, qt, keys, values, seen=None):
         top, acc = state
         s = jnp.dot(keys, qt, preferred_element_type=F32)
@@ -186,55 +227,44 @@
     def finish(j, acc):
         out_ref[j] = (acc[0:HD] / acc[HD : HD + 1]).astype(BF16)
 
-    def base_of(j):
-        return jnp.bitwise_and(j + start + BLOCKS, BLOCKS - 1)
-
     def in_window(edge_key, base):
         block = jnp.bitwise_and(lax.shift_right_logical(edge_key, 5), BLOCKS - 1)
         return jnp.bitwise_and(block - base + BLOCKS, BLOCKS - 1) < width
 
-    zero = jnp.zeros((ROWS, TOK), F32)
-
-    @pl.when(jnp.logical_and(safe, polar))
-    def _():
-        @pl.loop(0, BLOCKS, step=PAIR)
-        def _(first):
-            for j in (first + n for n in range(PAIR)):
-                qt = recv_ref[j, 0:HD, :]
-                acc = zero
-                for at, size in pieces(OWN):
-                    acc = plain(acc, qt, *own(at, size))
-                acc = plain(acc, qt, *halo(0, HALO))
-                finish(j, acc)
-
-    grain = 4
-    for count in range(grain, BLOCKS + 1, grain):
-        fits = jnp.logical_and(width <= count, width > count - grain)
-
-        @pl.when(jnp.logical_and(jnp.logical_and(safe, jnp.logical_not(polar)), fits))
+    def add_halo(j, acc, one_side):
+        qt = recv_ref[j, 0:HD, :]
+        if one_side:
+            acc = plain(acc, qt, *halo(0, HALO))
+        else:
+            lanes = lax.broadcasted_iota(jnp.int32, (1, 2 * HALO), 1)
+            acc = plain(acc, qt, *halo(0, 2 * HALO), in_window(lanes, window_base(j, start)))
+        finish(j, acc)
+
+    for one_side, here in ((True, polar), (False, jnp.logical_not(polar))):
+
+        @pl.when(jnp.logical_and(safe, here))
+        def _(one_side=one_side):
+            for j in range(PRE):
+                add_halo(j, pre_ref[j], one_side)
+
+    for count, fits in variants(width, polar):
+
+        @pl.when(jnp.logical_and(safe, fits))
         def _(count=count):
-            @pl.loop(0, BLOCKS, step=PAIR)
+            @pl.loop(PRE, BLOCKS, step=PAIR)
             def _(first):
                 for j in (first + n for n in range(PAIR)):
+                    base = None if count is None else window_base(j, start)
                     qt = recv_ref[j, 0:HD, :]
-                    base = base_of(j)
-                    acc = zero
-                    for at, size in pieces(count * TOK):
-                        seen = None
-                        if at + size > (count - grain + 1) * TOK:
-                            lanes = lax.broadcasted_iota(jnp.int32, (1, size), 1)
-                            seen = lanes < width * TOK - at
-                        acc = plain(acc, qt, *own(pl.multiple_of(base * TOK + at, TOK), size), seen)
-                    lanes = lax.broadcasted_iota(jnp.int32, (1, 2 * HALO), 1)
-                    acc = plain(acc, qt, *halo(0, 2 * HALO), in_window(lanes, base))
-                    finish(j, acc)
+                    acc = own_part(qt, base, width, count or BLOCKS, k_ref, vt_ref)
+                    add_halo(j, acc, count is None)
 
     @pl.when(jnp.logical_not(safe))
     def _():
         @pl.loop(0, BLOCKS)
         def _(j):
             qt = recv_ref[j, 0:HD, :]
-            base = base_of(j)
+            base = window_base(j, start)
 
             def own_step(n, state):
                 return shifted(state, qt, *own(pl.multiple_of((base + n) * TOK, TOK), TOK))
@@ -244,18 +274,18 @@
                 row = lax.broadcasted_iota(jnp.int32, (TOK, 1), 0) + at
                 return shifted(state, qt, *halo(at, TOK), in_window(row, base))
 
-            state = (jnp.full((1, TOK), NEG, F32), zero)
+            state = (jnp.full((1, TOK), NEG, F32), jnp.zeros((ROWS, TOK), F32))
             state = lax.fori_loop(0, width, own_step, state)
             sides = jnp.where(polar, HALO // TOK, 2 * HALO // TOK)
             state = lax.fori_loop(0, sides, halo_step, state)
             finish(j, state[1])
 
 
-def attend(scalars, peaks, recv, keys, values, side_a, side_b):
+def attend(scalars, peaks, recv, keys, values, pre, side_a, side_b):
     return pl.pallas_call(
         attend_kernel,
         out_shape=jax.ShapeDtypeStruct((BLOCKS, HD, TOK), BF16),
-        in_specs=[SMEM, SMEM] + [VMEM] * 5,
+        in_specs=[SMEM, SMEM] + [VMEM] * 6,
         out_specs=VMEM,
         scratch_shapes=[
             pltpu.VMEM((2 * HALO, HD), BF16),
@@ -266,7 +296,7 @@
             flops=4 * OWN * OWN * HD, bytes_accessed=8 << 20, transcendentals=OWN * OWN
         ),
         name="attend",
-    )(scalars, peaks, recv, keys, values, side_a, side_b)
+    )(scalars, peaks, recv, keys, values, pre, side_a, side_b)
 
 
 def mix_kernel(att_ref, wo_ref, x_ref, out_ref):
@@ -308,8 +338,8 @@
     pairs_b = [(b, ((b - 1) ^ 1) + 1) for b in range(1, n_lat - 1)]
     side_a = lax.ppermute(side_a, "lat", pairs_a)
     side_b = lax.ppermute(side_b, "lat", pairs_b)
-    keys, values, peaks = prepare(scalars, recv)
-    att = swap(attend(scalars, peaks, recv, keys, values, side_a, side_b))
+    keys, values, peaks, pre = prepare(scalars, recv)
+    att = swap(attend(scalars, peaks, recv, keys, values, pre, side_a, side_b))
     return mix(att.reshape(width, -1), o_weight, tokens)
 
 

time: 176 us -> 176 us (level)
  no operation moved by 1% of the time
where the time goes in v3:
time: 176 us
  Pallas kernels  125 us (71%)
  waiting for transfers between devices  21.3 us (12%)
  blocking collectives  17.8 us (10%)
  starting transfers between devices  9.63 us (5%)
  local copies, waits for them, and re-layouts  2.53 us (1%)
    pallas_call x1, Pallas kernels, attend(): pl.pallas_call(attend_kernel, out_shape=jax.ShapeDtypeStruct((BLOCKS, HD,...  115 us
    all_to_all x1, waiting for transfers between devices, swap(): return lax.all_to_all(value, 'lon', split_axis=0, concat_axis=0, tiled=True)  20.2 us
    all_to_all x1, blocking collectives, swap(): return lax.all_to_all(value, 'lon', split_axis=0, concat_axis=0, tiled=True)  17.8 us
    all_to_all x1, starting transfers between devices, swap(): return lax.all_to_all(value, 'lon', split_axis=0, concat_axis=0, tiled=True)  8.57 us
    pallas_call x1, Pallas kernels, project(): pl.pallas_call(project_kernel, grid=(steps,), out_shape=jax.ShapeDtypeStr...  5.8 us
  transfers between devices with their start and end apart: 3, of which 2 were waited for; matrix products, arithmetic and copies ran while one was open for 1% of the time, Pallas kernels for 1%

profile of v3, /device:TPU:1, one launch (start us, length us, event | category | flops | bytes accessed | tf_op | source)
XLA Modules:
  0.0 176.2 jit_solution(14240358411245416282)
XLA Ops:
  0.0 5.8 %project.1 = bf16[16,192,256]{2,1,0:T(8,128)(2,1)} custom-call(bf16[8,16,2,1024]{3,2,1,0:T(2,128)(2,1)} %x_ref.3, bf16[1024]{0:T(1024)(128)(2,1)} %gain_ref.1, bf16[1024,1024]{1,0:T(8,128)(2,1)} %wq_ref.1, bf16[1024,1024]{1,0:T(8,128)(2,1)} %wk_ref.1, bf16[1024,1024]{1,0:T(8,128)(2,1)} %wv_ref.1), custom_call_target="tpu_custom_call" | custom-call | tf_op jit(solution)/shard_map/project/pallas_call | solution.py:54
  5.8 0.0 copy-start.2
  5.8 0.0 copy-start.3
  5.8 8.6 %all-to-all-start = ((bf16[16,192,256]{2,1,0:T(8,128)(2,1)}), bf16[16,192,256]{2,1,0:T(8,128)(2,1)S(1)}, u32[]{:S(2)}, u32[]{:S(2)}) async-start(bf16[16,192,256]{2,1,0:T(8,128)(2,1)} %project.1), calls=%async_computation | async-start | bytes 3145728 | tf_op jit(solution)/shard_map/all_to_all | solution.py:325
  14.4 0.0 copy-done.2
  14.4 0.6 dynamic_slice.7
  15.0 0.0 copy-done.3
  15.0 0.6 dynamic_slice.6
  15.6 1.3 stack.11.scal_ref
  16.9 20.2 %all-to-all-done.recv_ref = bf16[16,192,256]{2,1,0:T(8,128)(2,1)S(1)} async-done(((bf16[16,192,256]{2,1,0:T(8,128)(2,1)}), bf16[16,192,256]{2,1,0:T(8,128)(2,1)S(1)}, u32[]{:S(2)}, u32[]{:S(2)}) %all-to-all-start) | async-done | bytes 1572896 | tf_op jit(solution)/shard_map/all_to_all | solution.py:325
  37.1 0.9 edges.1
  38.0 0.4 collective-permute-start
  38.4 0.7 collective-permute-start.1
  39.0 1.7 prepare.1
  40.8 1.1 collective-permute-done.a_ref
  41.9 0.0 collective-permute-done.1.b_ref
  41.9 0.0 copy-start
  41.9 0.0 copy-start.1
  41.9 114.9 %attend.1 = bf16[16,64,256]{2,1,0:T(8,128)(2,1)S(1)} custom-call(s32[5]{0:T(128)S(1)} %stack.11.scal_ref, f32[1,2]{1,0:T(1,128)S(1)} %get-tuple-element.11.peak_ref, bf16[16,192,256]{2,1,0:T(8,128)(2,1)S(1)} %all-to-all-done.recv_ref, bf16[8192,64]{1,0:T(8,128)(2,1)S(1)} %get-tuple-element.12.k_ref, bf16[80,8192]{1,0:T(8,128)(2,1)S(1)} %get-tuple-element.13.vt_ref, ...), custom_call_target="tpu_custom_call" | custom-call | flops 4294967296 | bytes 8388608 | tf_op jit(solution)/shard_map/attend/pallas_call | solution.py:285
  156.8 17.8 %all_to_all.10 = bf16[16,64,256]{2,1,0:T(8,128)(2,1)S(1)} all-to-all(bf16[16,64,256]{2,1,0:T(8,128)(2,1)S(1)} %attend.1), channel_id=1, replica_groups=mesh['lat'=16,'lon'=16] {'lon'}, dimensions={0} | all-to-all | bytes 1048576 | tf_op jit(solution)/shard_map/all_to_all | solution.py:325
  174.6 0.0 copy-done
  174.6 0.0 copy-done.1
  174.6 1.6 mix.1
Async XLA Ops:
  5.8 8.6 %copy-start.2 = (s32[16]{0:T(128)S(1)}, s32[16]{0:T(128)}, u32[]{:S(2)}) copy-start(s32[16]{0:T(128)} %param.15) | copy-start | bytes 196
  5.8 9.1 %copy-start.3 = (s32[16]{0:T(128)S(1)}, s32[16]{0:T(128)}, u32[]{:S(2)}) copy-start(s32[16]{0:T(128)} %param.14) | copy-start | bytes 196
  5.8 31.3 %all-to-all-start = ((bf16[16,192,256]{2,1,0:T(8,128)(2,1)}), bf16[16,192,256]{2,1,0:T(8,128)(2,1)S(1)}, u32[]{:S(2)}, u32[]{:S(2)}) async-start(bf16[16,192,256]{2,1,0:T(8,128)(2,1)} %project.1), calls=%async_computation | async-start | bytes 3145728 | tf_op jit(solution)/shard_map/all_to_all | solution.py:325
  38.0 3.9 %collective-permute-start = (bf16[512,128]{1,0:T(8,128)(2,1)S(1)}, bf16[512,128]{1,0:T(8,128)(2,1)S(1)}, u32[]{:S(2)}, u32[]{:S(2)}) collective-permute-start(bf16[512,128]{1,0:T(8,128)(2,1)S(1)} %get-tuple-element.15), channel_id=1, source_target_pairs={{0,16},{16,0},{32,48},{48,32},{64,80},{80,64},{96,112},{112,96},{1... | collective-permute-start | bytes 393224 | tf_op jit(solution)/shard_map/ppermute | solution.py:339
  38.4 3.5 %collective-permute-start.1 = (bf16[512,128]{1,0:T(8,128)(2,1)S(1)}, bf16[512,128]{1,0:T(8,128)(2,1)S(1)}, u32[]{:S(2)}, u32[]{:S(2)}) collective-permute-start(bf16[512,128]{1,0:T(8,128)(2,1)S(1)} %get-tuple-element.16), channel_id=1, source_target_pairs={{16,32},{32,16},{48,64},{64,48},{80,96},{96,80},{112,128},{128,112... | collective-permute-start | bytes 393224 | tf_op jit(solution)/shard_map/ppermute | solution.py:340
  41.9 132.7 %copy-start = (bf16[8,16,2,1024]{3,2,1,0:T(2,128)(2,1)S(1)}, bf16[8,16,2,1024]{3,2,1,0:T(2,128)(2,1)}, u32[]{:S(2)}) copy-start(bf16[8,16,2,1024]{3,2,1,0:T(2,128)(2,1)} %x_ref.3) | copy-start | bytes 1572868
  41.9 132.7 %copy-start.1 = (bf16[1024,1024]{1,0:T(8,128)(2,1)S(1)}, bf16[1024,1024]{1,0:T(8,128)(2,1)}, u32[]{:S(2)}) copy-start(bf16[1024,1024]{1,0:T(8,128)(2,1)} %wo_ref.1) | copy-start | bytes 6291460

commit v4 on v3

--- a/solution.py
+++ b/solution.py
@@ -155,17 +155,24 @@
         k_most = jnp.maximum(k_most, jnp.sum(kf * kf, 0, keepdims=True))
         v = (recv_ref[j, 2 * HD :, :].astype(F32) * times).astype(BF16)
         kt = k.T
-        for copy in range(2):
-            at = (copy * BLOCKS + j) * TOK
-            k_ref[at : at + TOK, :] = kt
-            vt_ref[0:HD, at : at + TOK] = v
-            vt_ref[HD:, at : at + TOK] = ones
+        at = j * TOK
+        k_ref[at : at + TOK, :] = kt
+        vt_ref[0:HD, at : at + TOK] = v
+        vt_ref[HD:, at : at + TOK] = ones
     q_peak = jnp.max(q_most)
     k_peak = jnp.max(k_most)
     peak_ref[0, 0] = q_peak
     peak_ref[0, 1] = k_peak
     safe = q_peak * k_peak < SAFE * SAFE
-    for count, fits in variants(width, jnp.logical_or(first, final)):
+    polar = jnp.logical_or(first, final)
+
+    @pl.when(jnp.logical_not(jnp.logical_and(safe, polar)))
+    def _():
+        for at in range(0, OWN, TOK):
+            k_ref[OWN + at : OWN + at + TOK, :] = k_ref[at : at + TOK, :]
+            vt_ref[:, OWN + at : OWN + at + TOK] = vt_ref[:, at : at + TOK]
+
+    for count, fits in variants(width, polar):
 
         @pl.when(jnp.logical_and(safe, fits))
         def _(count=count):

time: 176 us -> 176 us (level)
  no operation moved by 1% of the time
where the time goes in v4:
time: 176 us
  Pallas kernels  125 us (71%)
  waiting for transfers between devices  21.2 us (12%)
  blocking collectives  17.8 us (10%)
  starting transfers between devices  9.63 us (5%)
  local copies, waits for them, and re-layouts  2.53 us (1%)
    pallas_call x1, Pallas kernels, attend(): pl.pallas_call(attend_kernel, out_shape=jax.ShapeDtypeStruct((BLOCKS, HD,...  115 us
    all_to_all x1, waiting for transfers between devices, swap(): return lax.all_to_all(value, 'lon', split_axis=0, concat_axis=0, tiled=True)  20.2 us
    all_to_all x1, blocking collectives, swap(): return lax.all_to_all(value, 'lon', split_axis=0, concat_axis=0, tiled=True)  17.8 us
    all_to_all x1, starting transfers between devices, swap(): return lax.all_to_all(value, 'lon', split_axis=0, concat_axis=0, tiled=True)  8.57 us
    pallas_call x1, Pallas kernels, project(): pl.pallas_call(project_kernel, grid=(steps,), out_shape=jax.ShapeDtypeStr...  5.8 us
  transfers between devices with their start and end apart: 3, of which 2 were waited for; matrix products, arithmetic and copies ran while one was open for 1% of the time, Pallas kernels for 1%

profile of v4, /device:TPU:1, one launch (start us, length us, event | category | flops | bytes accessed | tf_op | source)
XLA Modules:
  0.0 176.2 jit_solution(13599821097220394206)
XLA Ops:
  0.0 5.8 %project.1 = bf16[16,192,256]{2,1,0:T(8,128)(2,1)} custom-call(bf16[8,16,2,1024]{3,2,1,0:T(2,128)(2,1)} %x_ref.3, bf16[1024]{0:T(1024)(128)(2,1)} %gain_ref.1, bf16[1024,1024]{1,0:T(8,128)(2,1)} %wq_ref.1, bf16[1024,1024]{1,0:T(8,128)(2,1)} %wk_ref.1, bf16[1024,1024]{1,0:T(8,128)(2,1)} %wv_ref.1), custom_call_target="tpu_custom_call" | custom-call | tf_op jit(solution)/shard_map/project/pallas_call | solution.py:54
  5.8 0.0 copy-start.2
  5.8 0.0 copy-start.3
  5.8 8.6 %all-to-all-start = ((bf16[16,192,256]{2,1,0:T(8,128)(2,1)}), bf16[16,192,256]{2,1,0:T(8,128)(2,1)S(1)}, u32[]{:S(2)}, u32[]{:S(2)}) async-start(bf16[16,192,256]{2,1,0:T(8,128)(2,1)} %project.1), calls=%async_computation | async-start | bytes 3145728 | tf_op jit(solution)/shard_map/all_to_all | solution.py:332
  14.4 0.0 copy-done.2
  14.4 0.6 dynamic_slice.7
  15.0 0.0 copy-done.3
  15.0 0.6 dynamic_slice.6
  15.6 1.3 stack.11.scal_ref
  16.9 20.2 %all-to-all-done.recv_ref = bf16[16,192,256]{2,1,0:T(8,128)(2,1)S(1)} async-done(((bf16[16,192,256]{2,1,0:T(8,128)(2,1)}), bf16[16,192,256]{2,1,0:T(8,128)(2,1)S(1)}, u32[]{:S(2)}, u32[]{:S(2)}) %all-to-all-start) | async-done | bytes 1572896 | tf_op jit(solution)/shard_map/all_to_all | solution.py:332
  37.1 0.9 edges.1
  38.0 0.4 collective-permute-start
  38.4 0.7 collective-permute-start.1
  39.0 1.9 %prepare.1 = (bf16[8192,64]{1,0:T(8,128)(2,1)S(1)}, bf16[80,8192]{1,0:T(8,128)(2,1)S(1)}, f32[1,2]{1,0:T(1,128)S(1)}, f32[2,80,256]{2,1,0:T(8,128)S(1)}) custom-call(s32[5]{0:T(128)S(1)} %stack.11.scal_ref, bf16[16,192,256]{2,1,0:T(8,128)(2,1)S(1)} %all-to-all-done.recv_ref), custom_call_target="tpu_custom_call" | custom-call | flops 1000000000 | bytes 6291456 | tf_op jit(solution)/shard_map/prepare/pallas_call | solution.py:186
  40.9 1.0 collective-permute-done.a_ref
  41.9 0.0 collective-permute-done.1.b_ref
  41.9 0.0 copy-start
  41.9 0.0 copy-start.1
  41.9 114.9 %attend.1 = bf16[16,64,256]{2,1,0:T(8,128)(2,1)S(1)} custom-call(s32[5]{0:T(128)S(1)} %stack.11.scal_ref, f32[1,2]{1,0:T(1,128)S(1)} %get-tuple-element.11.peak_ref, bf16[16,192,256]{2,1,0:T(8,128)(2,1)S(1)} %all-to-all-done.recv_ref, bf16[8192,64]{1,0:T(8,128)(2,1)S(1)} %get-tuple-element.12.k_ref, bf16[80,8192]{1,0:T(8,128)(2,1)S(1)} %get-tuple-element.13.vt_ref, ...), custom_call_target="tpu_custom_call" | custom-call | flops 4294967296 | bytes 8388608 | tf_op jit(solution)/shard_map/attend/pallas_call | solution.py:292
  156.8 17.8 %all_to_all.10 = bf16[16,64,256]{2,1,0:T(8,128)(2,1)S(1)} all-to-all(bf16[16,64,256]{2,1,0:T(8,128)(2,1)S(1)} %attend.1), channel_id=1, replica_groups=mesh['lat'=16,'lon'=16] {'lon'}, dimensions={0} | all-to-all | bytes 1048576 | tf_op jit(solution)/shard_map/all_to_all | solution.py:332
  174.6 0.0 copy-done
  174.6 0.0 copy-done.1
  174.6 1.6 mix.1
Async XLA Ops:
  5.8 8.6 %copy-start.2 = (s32[16]{0:T(128)S(1)}, s32[16]{0:T(128)}, u32[]{:S(2)}) copy-start(s32[16]{0:T(128)} %param.15) | copy-start | bytes 196
  5.8 9.1 %copy-start.3 = (s32[16]{0:T(128)S(1)}, s32[16]{0:T(128)}, u32[]{:S(2)}) copy-start(s32[16]{0:T(128)} %param.14) | copy-start | bytes 196
  5.8 31.3 %all-to-all-start = ((bf16[16,192,256]{2,1,0:T(8,128)(2,1)}), bf16[16,192,256]{2,1,0:T(8,128)(2,1)S(1)}, u32[]{:S(2)}, u32[]{:S(2)}) async-start(bf16[16,192,256]{2,1,0:T(8,128)(2,1)} %project.1), calls=%async_computation | async-start | bytes 3145728 | tf_op jit(solution)/shard_map/all_to_all | solution.py:332
  38.0 3.9 %collective-permute-start = (bf16[512,128]{1,0:T(8,128)(2,1)S(1)}, bf16[512,128]{1,0:T(8,128)(2,1)S(1)}, u32[]{:S(2)}, u32[]{:S(2)}) collective-permute-start(bf16[512,128]{1,0:T(8,128)(2,1)S(1)} %get-tuple-element.15), channel_id=1, source_target_pairs={{0,16},{16,0},{32,48},{48,32},{64,80},{80,64},{96,112},{112,96},{1... | collective-permute-start | bytes 393224 | tf_op jit(solution)/shard_map/ppermute | solution.py:346
  38.4 3.5 %collective-permute-start.1 = (bf16[512,128]{1,0:T(8,128)(2,1)S(1)}, bf16[512,128]{1,0:T(8,128)(2,1)S(1)}, u32[]{:S(2)}, u32[]{:S(2)}) collective-permute-start(bf16[512,128]{1,0:T(8,128)(2,1)S(1)} %get-tuple-element.16), channel_id=1, source_target_pairs={{16,32},{32,16},{48,64},{64,48},{80,96},{96,80},{112,128},{128,112... | collective-permute-start | bytes 393224 | tf_op jit(solution)/shard_map/ppermute | solution.py:347
  41.9 132.7 %copy-start = (bf16[8,16,2,1024]{3,2,1,0:T(2,128)(2,1)S(1)}, bf16[8,16,2,1024]{3,2,1,0:T(2,128)(2,1)}, u32[]{:S(2)}) copy-start(bf16[8,16,2,1024]{3,2,1,0:T(2,128)(2,1)} %x_ref.3) | copy-start | bytes 1572868
  41.9 132.7 %copy-start.1 = (bf16[1024,1024]{1,0:T(8,128)(2,1)S(1)}, bf16[1024,1024]{1,0:T(8,128)(2,1)}, u32[]{:S(2)}) copy-start(bf16[1024,1024]{1,0:T(8,128)(2,1)} %wo_ref.1) | copy-start | bytes 6291460
